TPU v7x, 32 devices: a whole 2x2x4 slice. The times are simulated.
32 devices in a mesh: row: 8 (over z, x), off: 4 (over y, core).
Axes of the slice: x: 2, y: 2, z: 4, core: 2. Of those that a mesh axis runs over, the one named last changes fastest.
Arguments:
- start_block: float32 [6, 1048576], P(None, ('row', 'off'))
- diagonal: float32 [1048576], P(('row', 'off')), may hold values from 2 to 6
- tile_values: float32 [8, 4, 80, 128, 128], P('row', 'off'), may hold values from -0.1875 to 0.1875
- tile_rows: int32 [8, 4, 80], P('row', 'off'), may hold values from 0 to 1023
- tile_cols: int32 [8, 4, 80], P('row', 'off'), may hold values from 0 to 1023
- tile_counts: int32 [8, 4], P('row', 'off'), may hold values from 20 to 80, as said below
- offset_map: int32 [4], replicated, may hold values from 0 to 3, as said below
Outputs:
- final_block: float32 [6, 1048576], P(None, ('row', 'off'))
- residual: float32 [6, 1048576], P(None, ('row', 'off'))
Inputs may be any that keep to these rules, and one draw needn't show every extreme that they name: `tile_counts`: live tiles of one device; some device has exactly 80. `offset_map`: each offset 0 to 3 is held by 4 / 4 off indices.
All inputs are finite; a program needn't handle non-finite values.
Results may differ from a plain program's by a relative error of at most 0.0003.
Values sent between devices are 32-bit elements; how exact they have to be, the bound alone decides.
No kernel may reach another device: no remote copies, remote signals or barrier semaphores. Data moves between devices by JAX's collectives and lax.ppermute only.
A program may use at most 64 MiB of HBM per device.

v0:
```python
import functools

import jax
import jax.numpy as jnp
from jax import lax
from jax.experimental import pallas as pl
from jax.experimental.pallas import tpu as pltpu
from jax.sharding import PartitionSpec as P


VMEM = pl.BlockSpec(memory_space=pltpu.VMEM)
SMEM = pl.BlockSpec(memory_space=pltpu.SMEM)
MIB = 1 << 20
BF16 = jnp.bfloat16
F32 = jnp.float32


def swap(x, axis, mask):
    n = lax.axis_size(axis)
    return lax.ppermute(x, axis, [(i, i ^ mask) for i in range(n)])


def shift(x, distance):
    n = lax.axis_size("row")
    return lax.ppermute(x, "row", [(i, (i + distance) % n) for i in range(n)])


def after(x, *others):
    return lax.optimization_barrier((x, *others))[0]


def bits_of(axis):
    return [1 << b for b in reversed(range(lax.axis_size(axis).bit_length() - 1))]


def gather_off(x, hold=()):
    pieces = {0: x}
    for bit in bits_of("off"):
        for m in list(pieces):
            source = after(pieces[m], *hold) if m and hold else pieces[m]
            pieces[m | bit] = swap(source, "off", bit)
    return [pieces[m] for m in sorted(pieces)]


def sum_step(x, axis, bit):
    return x + swap(x, axis, bit)


def pairs(vectors):
    return [(i, j) for i in range(vectors) for j in range(i + 1)]


def call(kernel, out_shape, operands, in_specs=None, limit=16, scratch=(), flops=0, **kw):
    many = isinstance(out_shape, tuple)
    moved = sum(x.size * x.dtype.itemsize for x in operands)
    return pl.pallas_call(
        kernel,
        out_shape=out_shape,
        in_specs=in_specs or [VMEM] * len(operands),
        out_specs=kw.pop("out_specs", (VMEM,) * len(out_shape) if many else VMEM),
        scratch_shapes=list(scratch),
        compiler_params=pltpu.CompilerParams(vmem_limit_bytes=limit * MIB),
        cost_estimate=pl.CostEstimate(flops=flops, bytes_accessed=moved, transcendentals=0),
        **kw,
    )(*operands)


def pack_kernel(vectors, blocks, x_ref, o_ref):
    width = o_ref.shape[-1]

    @pl.loop(0, blocks, unroll=8)
    def _(b):
        o_ref[pl.ds(b * vectors, vectors), :] = x_ref[:, pl.ds(pl.multiple_of(b * width, width), width)]


def inner_kernel(vectors, x_ref, d_ref, o_ref):
    blocks, width = d_ref.shape
    both = pairs(vectors)
    zero = jnp.zeros((8, width), F32)

    def step(c, sums):
        at = pl.multiple_of(c * 8, 8)
        d = d_ref[pl.ds(at, 8), :]
        x = [x_ref[pl.ds(at * vectors + v, 8, stride=vectors), :] for v in range(vectors)]
        y = [a * d for a in x]
        first = [s + x[i] * x[j] for s, (i, j) in zip(sums, both)]
        second = [s + x[i] * y[j] for s, (i, j) in zip(sums[len(both) :], both)]
        return tuple(first + second)

    sums = lax.fori_loop(0, blocks // 8, step, (zero,) * (2 * len(both)))
    for k, s in enumerate(sums):
        o_ref[pl.ds(8 * k, 8), :] = s


def divide_kernel(t_ref, hi_ref, lo_ref):
    t = t_ref[...]
    hi = t.astype(BF16)
    hi_ref[...] = hi
    lo_ref[...] = (t - hi.astype(F32)).astype(BF16)


def divide(tiles):
    slots, width, _ = tiles.shape
    step = max(s for s in (1, 2, 4, 8) if slots % s == 0)
    spec = pl.BlockSpec((step, width, width), lambda i: (i, 0, 0))
    shape = jax.ShapeDtypeStruct(tiles.shape, BF16)
    return call(
        divide_kernel, (shape, shape), (tiles,), [spec], 8,
        flops=tiles.size * 4, grid=(slots // step,), out_specs=(spec, spec),
    )


def pick_kernel(vectors, slots, where_ref, at_ref, *refs):
    pieces, outs = refs[:-2], refs[-2:]
    for which, out in enumerate(outs):

        @pl.loop(0, slots, unroll=4)
        def _(t):
            m = where_ref[which, t]
            at = at_ref[which, t]
            value = jnp.zeros((vectors, out.shape[-1]), F32)
            for k, piece in enumerate(pieces):
                value = jnp.where(m == k, piece[pl.ds(at, vectors), :], value)
            out[pl.ds(t * vectors, vectors), :] = value


def multiply_kernel(vectors, step, transposed, x_ref, hi_ref, lo_ref, o_ref):
    base = pl.program_id(0) * step
    width = x_ref.shape[-1]
    dims = (((1,), (1 if transposed else 0,)), ((), ()))

    def left(t):
        x = x_ref[pl.ds(t * vectors, vectors), :]
        x = jnp.concatenate([x, jnp.zeros((8 - vectors, width), F32)], axis=0)
        hi = x.astype(BF16).astype(F32)
        lo = x - hi
        top = jnp.concatenate([hi, hi], axis=1)
        low = jnp.concatenate([lo, jnp.zeros_like(lo)], axis=1)
        return [top, low]

    @pl.loop(0, step // 2, unroll=2)
    def _(p):
        i = 2 * p
        x = jnp.concatenate(left(base + i) + left(base + i + 1), axis=0).astype(BF16)
        along, across = (1, 0) if transposed else (0, 1)
        t = [jnp.concatenate([hi_ref[i + k], lo_ref[i + k]], axis=along) for k in (0, 1)]
        y = lax.dot_general(x, jnp.concatenate(t, axis=across), dims, preferred_element_type=F32)
        o_ref[pl.ds((base + i) * vectors, vectors), :] = (y[0:8, :width] + y[8:16, :width])[:vectors]
        o_ref[pl.ds((base + i + 1) * vectors, vectors), :] = (y[16:24, width:] + y[24:32, width:])[:vectors]


def multiply(x, high, low, ids, vectors, transposed, coupled=None):
    slots, width, _ = high.shape
    step = max(s for s in (2, 4, 8, 16, 20) if slots % s == 0)
    rows = vectors * slots
    spec = pl.BlockSpec((step, width, width), lambda i: (i, 0, 0))
    count = len(pairs(vectors))

    def kernel(x_ref, hi_ref, lo_ref, ids_ref, *refs):
        o_ref = refs[2] if coupled else refs[0]
        multiply_kernel(vectors, step, transposed, x_ref, hi_ref, lo_ref, o_ref)
        o_ref[pl.ds(rows, 8), :] = ids_ref[...]
        if coupled:

            @pl.when(pl.program_id(0) == pl.num_programs(0) - 1)
            def _():
                couple(vectors, slots, refs[0], o_ref, refs[1], refs[3])
                refs[4][...] = refs[3][...]

    out = jax.ShapeDtypeStruct((rows + 8, width), F32)
    if coupled:
        sums = jax.ShapeDtypeStruct((-(-2 * count // 8) * 8, width), F32)
        out = (out, sums, sums)
    operands = (x, high, low, ids) + (coupled or ())
    return call(
        kernel, out, operands, [VMEM, spec, spec] + [VMEM] * (len(operands) - 3), 12,
        flops=slots * 2 * 32 * 256 * 128, grid=(slots // step,),
    )


def couple(vectors, slots, x_ref, y_ref, p_ref, o_ref):
    both = pairs(vectors)
    n = len(both)

    def step(c, sums):
        at = pl.multiple_of(8 * c * vectors, 8)
        x = [x_ref[pl.ds(at + v, 8, stride=vectors), :] for v in range(vectors)]
        y = [y_ref[pl.ds(at + v, 8, stride=vectors), :] for v in range(vectors)]
        return tuple(s + (x[i] * y[j] + x[j] * y[i]) for s, (i, j) in zip(sums, both))

    sums = tuple(p_ref[pl.ds(8 * (n + k), 8), :] for k in range(n))
    sums = lax.fori_loop(0, slots // 8, step, sums)
    sums = [p_ref[pl.ds(8 * k, 8), :] for k in range(n)] + list(sums)
    for k, s in enumerate(sums):
        o_ref[k : k + 1, :] = jnp.sum(s, axis=0, keepdims=True)
    if o_ref.shape[0] > 2 * n:
        o_ref[2 * n :, :] = jnp.zeros((o_ref.shape[0] - 2 * n, o_ref.shape[1]), F32)
    total = jnp.sum(o_ref[...], axis=1, keepdims=True)
    o_ref[...] = jnp.broadcast_to(total, o_ref.shape)


def add_kernel(vectors, slots, blocks, started, me_ref, *refs):
    o_ref, lists = refs[-1], refs[:-1]
    if started:
        before, lists = lists[0], lists[1:]
    width = o_ref.shape[-1]
    row = lax.broadcasted_iota(jnp.int32, (blocks, width), 0) + me_ref[0] * blocks
    row = row.astype(F32)
    pad = jnp.zeros((width - slots, vectors * width), F32)
    sums = None
    for k in range(0, len(lists), 2):
        hots, blocks_of = [], []
        for ref in lists[k : k + 2]:
            ids = ref[vectors * slots : vectors * slots + 1, :]
            hots.append(jnp.where(ids == row, 1.0, 0.0).astype(BF16))
            y = [ref[pl.ds(v, slots, stride=vectors), :] for v in range(vectors)]
            blocks_of += [jnp.concatenate(y, axis=1), pad]
        hot = jnp.concatenate(hots, axis=1)
        y = jnp.concatenate(blocks_of, axis=0)
        hi = y.astype(BF16)
        lo = (y - hi.astype(F32)).astype(BF16)
        part = jnp.dot(hot, hi, preferred_element_type=F32) + jnp.dot(hot, lo, preferred_element_type=F32)
        sums = part if sums is None else sums + part
    for v in range(vectors):
        s = sums[:, v * width : (v + 1) * width]
        if started:
            s = s + before[pl.ds(v * blocks, blocks), :]
        o_ref[pl.ds(v * blocks, blocks), :] = s


def add_lists(me, lists, vectors, slots, blocks, before=None):
    width = lists[0].shape[-1]
    operands = (me,) + (() if before is None else (before,)) + tuple(lists)
    return call(
        functools.partial(add_kernel, vectors, slots, blocks, before is not None),
        jax.ShapeDtypeStruct((vectors * blocks, width), F32), operands,
        [SMEM] + [VMEM] * (len(operands) - 1), 16, flops=len(lists) * 2 * 256 * 256 * 768,
    )


def algebra(vectors, total, sums_ref):
    both = pairs(vectors)
    n = len(both)
    g, q = {}, {}
    for k, (i, j) in enumerate(both):
        g[i, j] = sums_ref[k : k + 1, :] * (1.0 / total)
        q[i, j] = q[j, i] = sums_ref[n + k : n + k + 1, :] * (1.0 / total)
    low, inv = {}, {}
    rev = []
    for j in range(vectors):
        s = g[j, j]
        for k in range(j):
            s = s - low[j, k] * low[j, k]
        rev.append(1.0 / jnp.sqrt(s))
        for i in range(j + 1, vectors):
            s = g[i, j]
            for k in range(j):
                s = s - low[i, k] * low[j, k]
            low[i, j] = s * rev[j]
    for j in range(vectors):
        inv[j, j] = rev[j]
        for i in range(j + 1, vectors):
            s = low[i, j] * inv[j, j]
            for k in range(j + 1, i):
                s = s + low[i, k] * inv[k, j]
            inv[i, j] = -s * rev[i]
    half, onto, proj = {}, {}, {}
    for i in range(vectors):
        for j in range(vectors):
            half[i, j] = sum(inv[i, k] * q[k, j] for k in range(i + 1))
    for i in range(vectors):
        for j in range(vectors):
            proj[i, j] = sum(half[i, k] * inv[j, k] for k in range(j + 1))
    for i in range(vectors):
        for j in range(vectors):
            onto[i, j] = sum(proj[i, k] * inv[k, j] for k in range(j, vectors))
    return inv, onto


def finish_kernel(vectors, total, steps, sums_ref, x_ref, d_ref, m_ref, final_ref, residual_ref, coef, res, fin):
    blocks, width = d_ref.shape
    chunk = blocks // steps
    start = pl.program_id(0) * chunk
    both = pairs(vectors)
    places = {("i", key): k for k, key in enumerate(both)}
    for i in range(vectors):
        for j in range(vectors):
            places["o", (i, j)] = len(places)

    @pl.when(pl.program_id(0) == 0)
    def _():
        inv, onto = algebra(vectors, total, sums_ref)
        for name, table in (("i", inv), ("o", onto)):
            for key in table:
                coef[pl.ds(8 * places[name, key], 8), :] = jnp.broadcast_to(table[key], (8, width))

    @pl.loop(0, chunk // 8, unroll=2)
    def _(c):
        local = pl.multiple_of(c * 8, 8)
        at = pl.multiple_of(start + local, 8)
        d = d_ref[pl.ds(at, 8), :]
        rd = 1.0 / d
        x = [x_ref[pl.ds(at * vectors + v, 8, stride=vectors), :] for v in range(vectors)]
        m = [m_ref[pl.ds(v * blocks + at, 8), :] + x[v] * d for v in range(vectors)]

        def value(name, i, j):
            return coef[pl.ds(8 * places[name, (i, j)], 8), :]

        for i in range(vectors):
            basis = r = None
            for j in range(i + 1):
                f = value("i", i, j)
                basis = f * x[j] if basis is None else basis + f * x[j]
                r = f * m[j] if r is None else r + f * m[j]
            for j in range(vectors):
                r = r - value("o", i, j) * x[j]
            res[pl.ds(8 * local + i, 8, stride=8), :] = r
            fin[pl.ds(8 * local + i, 8, stride=8), :] = basis - r * rd

    @pl.loop(0, chunk, unroll=8)
    def _(b):
        at = pl.multiple_of(b * width, width)
        residual_ref[:, pl.ds(at, width)] = res[pl.ds(pl.multiple_of(8 * b, 8), vectors), :]
        final_ref[:, pl.ds(at, width)] = fin[pl.ds(pl.multiple_of(8 * b, 8), vectors), :]


def body(start_block, diagonal, tile_values, tile_rows, tile_cols, tile_counts, offset_map):
    tiles = tile_values[0, 0]
    live_count = tile_counts[0, 0]
    row_size = lax.axis_size("row")
    off_size = lax.axis_size("off")
    me = lax.axis_index("off").astype(jnp.int32)
    offset = offset_map[me]
    vectors, shard = start_block.shape
    slots, width, _ = tiles.shape
    blocks = shard // width
    total = shard * off_size * row_size
    distances = range(row_size // 2)
    count = len(pairs(vectors))

    packed = call(
        functools.partial(pack_kernel, vectors, blocks),
        jax.ShapeDtypeStruct((vectors * blocks, width), F32), (start_block,),
    )
    live = jnp.arange(slots, dtype=jnp.int32) < live_count
    row_ids = jnp.where(live, tile_rows[0, 0], -1)
    col_ids = jnp.where(live, tile_cols[0, 0], -1)

    def padded(ids):
        return jnp.pad(ids.astype(F32)[None, :], ((0, 7), (0, width - slots)), constant_values=-1)

    row_line, col_line = padded(row_ids), padded(col_ids)
    group_line = lax.switch(
        offset,
        [functools.partial(lambda s, c: shift(c, s) if s else c, s) for s in distances],
        col_line,
    )
    both = jnp.stack([row_ids, group_line[0, :slots].astype(jnp.int32)])
    where = jnp.where(both < 0, -1, (both // blocks) ^ me)
    at = jnp.where(both < 0, 0, both % blocks) * vectors

    diagonal = diagonal.reshape(blocks, width)
    inner = call(
        functools.partial(inner_kernel, vectors),
        jax.ShapeDtypeStruct((16 * count, width), F32), (packed, diagonal),
    )
    high, low = divide(tiles)
    pieces = gather_off(packed, (where, at, inner, high, low))
    picked = jax.ShapeDtypeStruct((vectors * slots, width), F32)
    picked_row, picked_col = call(
        functools.partial(pick_kernel, vectors, slots), (picked, picked),
        (where, at, *pieces), [SMEM, SMEM] + [VMEM] * off_size,
    )

    row_bits, off_bits = bits_of("row")[::-1], bits_of("off")[::-1]

    def middle(s, picked_row, picked_col, high, low, row_line, col_line, inner):
        arrived = shift(picked_col, -s) if s else picked_col
        mirrored = multiply(picked_row, high, low, col_line, vectors, False)
        returned = shift(mirrored, s) if s else mirrored
        direct, sums, _ = multiply(arrived, high, low, row_line, vectors, True, (picked_row, inner))
        return direct, returned, sums

    direct, returned, sums = lax.switch(
        offset,
        [functools.partial(middle, s) for s in distances],
        picked_row, picked_col, high, low, row_line, col_line, inner,
    )
    stages = [sums]
    order = [("off", off_bits[-1])] + [("row", b) for b in row_bits] + [("off", b) for b in off_bits[:-1]]
    for axis, bit in order[:-1]:
        stages.append(sum_step(stages[-1], axis, bit))
    lists = []
    for a, b in zip(gather_off(direct, (stages[-2],)), gather_off(returned, (stages[-1],))):
        lists += [a, b]
    half = off_size
    image = add_lists(me[None], lists[:half], vectors, slots, blocks)
    sums = sum_step(stages[-1], *order[-1])
    image = add_lists(me[None], lists[half:], vectors, slots, blocks, image)
    out = jax.ShapeDtypeStruct((vectors, shard), F32)
    steps = 4 if blocks % 64 == 0 else 1
    spec = pl.BlockSpec((vectors, shard // steps), lambda i: (0, i))
    return call(
        functools.partial(finish_kernel, vectors, float(total), steps), (out, out),
        (sums, packed, diagonal, image), limit=24,
        scratch=(
            pltpu.VMEM((8 * (vectors * vectors + count), width), F32),
            pltpu.VMEM((8 * blocks // steps, width), F32),
            pltpu.VMEM((8 * blocks // steps, width), F32),
        ),
        grid=(steps,), out_specs=(spec, spec),
    )


def solution(mesh):
    return jax.shard_map(
        body,
        mesh=mesh,
        in_specs=(
            P(None, ("row", "off")),
            P(("row", "off")),
            P("row", "off", None, None, None),
            P("row", "off", None),
            P("row", "off", None),
            P("row", "off"),
            P(),
        ),
        out_specs=(P(None, ("row", "off")), P(None, ("row", "off"))),
        check_vma=False,
    )
```

profile of v0, /device:TPU:0, one launch (start us, length us, event | category | flops | bytes accessed | tf_op | source)
XLA Modules:
  0.0 76.7 jit_solution(15955947109637108674)
XLA Ops:
  0.6 1.2 %copy-done.1 = f32[6,32768]{1,0:T(8,128)S(1)} copy-done((f32[6,32768]{1,0:T(8,128)S(1)}, f32[6,32768]{1,0:T(8,128)}, u32[]{:S(2)}) %copy-start.1) | copy-done | bytes 786456
  1.9 0.4 shard_map.86.x_ref.refs_0_
  2.3 3.1 %collective-permute-start.10 = (f32[1536,128]{1,0:T(8,128)S(1)}, f32[1536,128]{1,0:T(8,128)S(1)}, u32[]{:S(2)}, u32[]{:S(2)}) collective-permute-start(f32[1536,128]{1,0:T(8,128)S(1)} %shard_map.86.x_ref.refs_0_), channel_id=1, source_target_pairs={{0,2},{1,3},{2,0},{3,1},{4,6},{5,7},{6,4},{7,5},{8,10},{9,11},{10,... | collective-permute-start | bytes 2359304 | tf_op jit(solution)/shard_map/ppermute | solution.py:20
  6.0 0.9 %copy-done.2 = f32[32768]{0:T(1024)S(1)} copy-done((f32[32768]{0:T(1024)S(1)}, f32[32768]{0:T(1024)}, u32[]{:S(2)}) %copy-start.2) | copy-done | bytes 131096
  6.9 0.8 %shard_map.87 = f32[336,128]{1,0:T(8,128)S(1)} custom-call(f32[1536,128]{1,0:T(8,128)S(1)} %shard_map.86.x_ref.refs_0_, f32[256,128]{1,0:T(8,128)S(1)} %bitcast.13), custom_call_target="tpu_custom_call" | custom-call | bytes 917504 | tf_op jit(solution)/shard_map/pallas_call | solution.py:56
  7.7 0.6 dynamic_slice.3
  9.0 6.5 %conditional.2 = (f32[8,128]{1,0:T(8,128)}) conditional(s32[]{:T(128)} %bitcast, f32[8,128]{1,0:T(8,128)S(1)} %pad.9, f32[8,128]{1,0:T(8,128)S(1)} %pad.9, f32[8,128]{1,0:T(8,128)S(1)} %pad.9, f32[8,128]{1,0:T(8,128)S(1)} %pad.9), branch_computations={%region_0.1_spmd, %region_1.2_spmd, %region_2.3_spmd, %region_3.4_... | conditional | bytes 16432 | solution.py:353
  9.0 1.5 %collective-permute-start = (f32[8,128]{1,0:T(8,128)S(1)}, f32[8,128]{1,0:T(8,128)}, u32[]{:S(2)}, u32[]{:S(2)}) collective-permute-start(f32[8,128]{1,0:T(8,128)S(1)} %param.1), channel_id=1, source_target_pairs={{0,4},{4,8},{8,12},{12,16},{16,20},{20,24},{24,28},{28,0},{1,5},{5... | collective-permute-start | bytes 12296 | tf_op jit(solution)/shard_map/cond/branch_1_fun/ppermute | solution.py:25
  10.5 4.9 %collective-permute-done = f32[8,128]{1,0:T(8,128)} collective-permute-done((f32[8,128]{1,0:T(8,128)S(1)}, f32[8,128]{1,0:T(8,128)}, u32[]{:S(2)}, u32[]{:S(2)}) %collective-permute-start) | collective-permute-done | bytes 4128 | tf_op jit(solution)/shard_map/cond/branch_1_fun/ppermute | solution.py:25
  15.5 2.5 %copy-done = f32[1,1,80,128,128]{4,3,2,1,0:T(8,128)S(1)} copy-done((f32[1,1,80,128,128]{4,3,2,1,0:T(8,128)S(1)}, f32[1,1,80,128,128]{4,3,2,1,0:T(8,128)}, u32[]{:S(2)}) %copy-start) | copy-done | bytes 5242904
  17.9 0.9 %shard_map.88 = (bf16[80,128,128]{2,1,0:T(8,128)(2,1)S(1)}, bf16[80,128,128]{2,1,0:T(8,128)(2,1)S(1)}) custom-call(f32[80,128,128]{2,1,0:T(8,128)S(1)} %bitcast.12), custom_call_target="tpu_custom_call" | custom-call | flops 5242880 | bytes 5242880 | tf_op jit(solution)/shard_map/pallas_call | solution.py:56
  18.9 0.7 slice_convert_fusion
  19.6 3.3 %collective-permute-done.10.refs_2_ = f32[1536,128]{1,0:T(8,128)S(1)} collective-permute-done((f32[1536,128]{1,0:T(8,128)S(1)}, f32[1536,128]{1,0:T(8,128)S(1)}, u32[]{:S(2)}, u32[]{:S(2)}) %collective-permute-start.10) | collective-permute-done | bytes 786464 | tf_op jit(solution)/shard_map/ppermute | solution.py:20
  22.9 2.3 %collective-permute-done.11.refs_3_ = f32[1536,128]{1,0:T(8,128)S(1)} collective-permute-done((f32[1536,128]{1,0:T(8,128)S(1)}, f32[1536,128]{1,0:T(8,128)S(1)}, u32[]{:S(2)}, u32[]{:S(2)}) %collective-permute-start.11) | collective-permute-done | bytes 786464 | tf_op jit(solution)/shard_map/ppermute | solution.py:20
  25.2 1.7 %shard_map.89 = (f32[480,128]{1,0:T(8,128)S(1)}, f32[480,128]{1,0:T(8,128)S(1)}) custom-call(s32[2,80]{1,0:T(2,128)S(1)} %get-tuple-element.126.where_ref, s32[2,80]{1,0:T(2,128)S(1)} %get-tuple-element.125.at_ref, f32[1536,128]{1,0:T(8,128)S(1)} %shard_map.86.x_ref.refs_0_, f32[1536,128]{1,0:T(8,128)S(1)} %collective-permute-done.9.refs_1_, ...), custom_call_target="tpu_custom_call" | custom-call | bytes 3147008 | tf_op jit(solution)/shard_map/pallas_call | solution.py:56
  26.9 17.7 %conditional.3 = (f32[488,128]{1,0:T(8,128)S(1)}, f32[488,128]{1,0:T(8,128)}, f32[48,128]{1,0:T(8,128)S(1)}) conditional(s32[]{:T(128)} %bitcast, (f32[480,128]{1,0:T(8,128)S(1)}, bf16[80,128,128]{2,1,0:T(8,128)(2,1)S(1)}, bf16[80,128,128]{2,1,0:T(8,128)(2,1)S(1)}, f32[8,128]{1,0:T(8,128)S(1)}, ...), branch_computations={%region_4.5_spmd, %region_5.6_spmd, %region_6.7_spmd, %region_7.8_... | conditional | flops 335544320 | bytes 13385832 | solution.py:384
  26.9 4.8 %collective-permute-start.3 = (f32[480,128]{1,0:T(8,128)S(1)}, f32[480,128]{1,0:T(8,128)S(1)}, u32[]{:S(2)}, u32[]{:S(2)}) collective-permute-start(f32[480,128]{1,0:T(8,128)S(1)} %get-tuple-element.74), channel_id=1, source_target_pairs={{0,28},{4,0},{8,4},{12,8},{16,12},{20,16},{24,20},{28,24},{1,29},{... | collective-permute-start | bytes 737288 | tf_op jit(solution)/shard_map/cond/branch_1_fun/ppermute | solution.py:25
  31.7 3.1 %branch_1_fun.3 = f32[488,128]{1,0:T(8,128)S(1)} custom-call(f32[480,128]{1,0:T(8,128)S(1)} %get-tuple-element.78.refs_0_.x_ref, bf16[80,128,128]{2,1,0:T(8,128)(2,1)S(1)} %get-tuple-element.75.hi_ref, bf16[80,128,128]{2,1,0:T(8,128)(2,1)S(1)} %get-tuple-element.76.lo_ref, f32[8,128]{1,0:T(8,128)S(1)} %get-tuple-element.81.ids_ref), custom_call_target="tpu_custom_call" | custom-call | flops 167772160 | bytes 5492736 | tf_op jit(solution)/shard_map/cond/branch_1_fun/pallas_call | solution.py:56
  34.9 3.2 %collective-permute-done.3.x_ref = f32[480,128]{1,0:T(8,128)S(1)} collective-permute-done((f32[480,128]{1,0:T(8,128)S(1)}, f32[480,128]{1,0:T(8,128)S(1)}, u32[]{:S(2)}, u32[]{:S(2)}) %collective-permute-start.3) | collective-permute-done | bytes 245792 | tf_op jit(solution)/shard_map/cond/branch_1_fun/ppermute | solution.py:25
  38.1 4.7 %branch_1_fun.2 = (f32[488,128]{1,0:T(8,128)S(1)}, f32[48,128]{1,0:T(8,128)S(1)}, f32[48,128]{1,0:T(8,128)}) custom-call(f32[480,128]{1,0:T(8,128)S(1)} %collective-permute-done.3.x_ref, bf16[80,128,128]{2,1,0:T(8,128)(2,1)S(1)} %get-tuple-element.75.hi_ref, bf16[80,128,128]{2,1,0:T(8,128)(2,1)S(1)} %get-tuple-element.76.lo_ref, ...), custom_call_target="tpu_custom_call" | custom-call | flops 167772160 | bytes 5910528 | tf_op jit(solution)/shard_map/cond/branch_1_fun/pallas_call | solution.py:56
  42.8 1.7 %collective-permute-done.4 = f32[488,128]{1,0:T(8,128)} collective-permute-done((f32[488,128]{1,0:T(8,128)S(1)}, f32[488,128]{1,0:T(8,128)}, u32[]{:S(2)}, u32[]{:S(2)}) %collective-permute-start.4) | collective-permute-done | bytes 249888 | tf_op jit(solution)/shard_map/cond/branch_1_fun/ppermute | solution.py:25
  44.6 2.0 %collective-permute-start.19 = (f32[488,128]{1,0:T(8,128)S(1)}, f32[488,128]{1,0:T(8,128)S(1)}, u32[]{:S(2)}, u32[]{:S(2)}) collective-permute-start(f32[488,128]{1,0:T(8,128)S(1)} %get-tuple-element.119.refs_0_), channel_id=1, source_target_pairs={{0,2},{1,3},{2,0},{3,1},{4,6},{5,7},{6,4},{7,5},{8,10},{9,11},{10,... | collective-permute-start | bytes 749576 | tf_op jit(solution)/shard_map/ppermute | solution.py:20
  46.6 10.6 %collective-permute-done.12 = f32[48,128]{1,0:T(8,128)S(1)} collective-permute-done((f32[48,128]{1,0:T(8,128)S(1)}, f32[48,128]{1,0:T(8,128)S(1)}, u32[]{:S(2)}, u32[]{:S(2)}) %collective-permute-start.12) | collective-permute-done | bytes 24608 | tf_op jit(solution)/shard_map/ppermute | solution.py:20
  57.2 3.8 %collective-permute-done.13 = f32[48,128]{1,0:T(8,128)S(1)} collective-permute-done((f32[48,128]{1,0:T(8,128)S(1)}, f32[48,128]{1,0:T(8,128)S(1)}, u32[]{:S(2)}, u32[]{:S(2)}) %collective-permute-start.13) | collective-permute-done | bytes 24608 | tf_op jit(solution)/shard_map/ppermute | solution.py:20
  61.1 0.5 collective-permute-start.18
  61.6 3.2 %collective-permute-done.14 = f32[48,128]{1,0:T(8,128)S(1)} collective-permute-done((f32[48,128]{1,0:T(8,128)S(1)}, f32[48,128]{1,0:T(8,128)S(1)}, u32[]{:S(2)}, u32[]{:S(2)}) %collective-permute-start.14) | collective-permute-done | bytes 24608 | tf_op jit(solution)/shard_map/ppermute | solution.py:20
  64.9 4.7 %collective-permute-done.15 = f32[48,128]{1,0:T(8,128)S(1)} collective-permute-done((f32[48,128]{1,0:T(8,128)S(1)}, f32[48,128]{1,0:T(8,128)S(1)}, u32[]{:S(2)}, u32[]{:S(2)}) %collective-permute-start.15) | collective-permute-done | bytes 24608 | tf_op jit(solution)/shard_map/ppermute | solution.py:20
  69.7 0.5 collective-permute-start.21
  70.3 1.3 %collective-permute-done.16 = f32[48,128]{1,0:T(8,128)S(1)} collective-permute-done((f32[48,128]{1,0:T(8,128)S(1)}, f32[48,128]{1,0:T(8,128)S(1)}, u32[]{:S(2)}, u32[]{:S(2)}) %collective-permute-start.16) | collective-permute-done | bytes 24608 | tf_op jit(solution)/shard_map/ppermute | solution.py:20
  71.6 1.5 %shard_map.90.refs_0_ = f32[1536,128]{1,0:T(8,128)S(1)} custom-call(s32[1]{0:T(128)} %bitcast.6.me_ref, f32[488,128]{1,0:T(8,128)S(1)} %get-tuple-element.119.refs_0_, f32[488,128]{1,0:T(8,128)} %get-tuple-element.120.refs_1_, f32[488,128]{1,0:T(8,128)S(1)} %collective-permute-done.17.refs_2_, f32[488,128]{1,0:T(8,128)S(1)} %collective-permute-done.18.refs_3_), custom_call_target="tpu_custom_call" | custom-call | flops 402653184 | bytes 999428 | tf_op jit(solution)/shard_map/pallas_call | solution.py:56
  73.2 0.6 shard_map.91.m_ref
  73.8 2.9 %shard_map.92 = (f32[6,32768]{1,0:T(8,128)}, f32[6,32768]{1,0:T(8,128)}) custom-call(f32[48,128]{1,0:T(8,128)S(1)} %add.35.sums_ref, f32[1536,128]{1,0:T(8,128)S(1)} %shard_map.86.x_ref.refs_0_, f32[256,128]{1,0:T(8,128)S(1)} %bitcast.14, f32[1536,128]{1,0:T(8,128)S(1)} %shard_map.91.m_ref), custom_call_target="tpu_custom_call" | custom-call | bytes 1728512 | tf_op jit(solution)/shard_map/pallas_call | solution.py:56
  (39 shorter events, 0.4 us)
Async XLA Ops:
  0.6 1.2 %copy-start.1 = (f32[6,32768]{1,0:T(8,128)S(1)}, f32[6,32768]{1,0:T(8,128)}, u32[]{:S(2)}) copy-start(f32[6,32768]{1,0:T(8,128)} %x_ref.1) | copy-start | bytes 2359300
  1.9 5.8 %copy-start.5 = (s32[4]{0:T(128)S(1)}, s32[4]{0:T(128)}, u32[]{:S(2)}) copy-start(s32[4]{0:T(128)} %param.21) | copy-start | bytes 52
  1.9 6.4 %copy-start.6 = (s32[1,1,80]{2,1,0:T(1,128)S(1)}, s32[1,1,80]{2,1,0:T(1,128)}, u32[]{:S(2)}) copy-start(s32[1,1,80]{2,1,0:T(1,128)} %param.19) | copy-start | bytes 964
  2.3 20.6 %collective-permute-start.10 = (f32[1536,128]{1,0:T(8,128)S(1)}, f32[1536,128]{1,0:T(8,128)S(1)}, u32[]{:S(2)}, u32[]{:S(2)}) collective-permute-start(f32[1536,128]{1,0:T(8,128)S(1)} %shard_map.86.x_ref.refs_0_), channel_id=1, source_target_pairs={{0,2},{1,3},{2,0},{3,1},{4,6},{5,7},{6,4},{7,5},{8,10},{9,11},{10,... | collective-permute-start | bytes 2359304 | tf_op jit(solution)/shard_map/ppermute | solution.py:20
  5.4 17.6 %collective-permute-start.9 = (f32[1536,128]{1,0:T(8,128)S(1)}, f32[1536,128]{1,0:T(8,128)S(1)}, u32[]{:S(2)}, u32[]{:S(2)}) collective-permute-start(f32[1536,128]{1,0:T(8,128)S(1)} %shard_map.86.x_ref.refs_0_), channel_id=1, source_target_pairs={{0,1},{1,0},{2,3},{3,2},{4,5},{5,4},{6,7},{7,6},{8,9},{9,8},{10,11... | collective-permute-start | bytes 2359304 | tf_op jit(solution)/shard_map/ppermute | solution.py:20
  6.0 0.9 %copy-start.2 = (f32[32768]{0:T(1024)S(1)}, f32[32768]{0:T(1024)}, u32[]{:S(2)}) copy-start(f32[32768]{0:T(1024)} %param.16) | copy-start | bytes 393220
  9.0 6.5 %collective-permute-start = (f32[8,128]{1,0:T(8,128)S(1)}, f32[8,128]{1,0:T(8,128)}, u32[]{:S(2)}, u32[]{:S(2)}) collective-permute-start(f32[8,128]{1,0:T(8,128)S(1)} %param.1), channel_id=1, source_target_pairs={{0,4},{4,8},{8,12},{12,16},{16,20},{20,24},{24,28},{28,0},{1,5},{5... | collective-permute-start | bytes 12296 | tf_op jit(solution)/shard_map/cond/branch_1_fun/ppermute | solution.py:25
  15.5 2.5 %copy-start = (f32[1,1,80,128,128]{4,3,2,1,0:T(8,128)S(1)}, f32[1,1,80,128,128]{4,3,2,1,0:T(8,128)}, u32[]{:S(2)}) copy-start(f32[1,1,80,128,128]{4,3,2,1,0:T(8,128)} %param.17) | copy-start | bytes 15728644
  17.9 0.9 %copy-start.4 = (s32[1,1,80]{2,1,0:T(1,128)S(1)}, s32[1,1,80]{2,1,0:T(1,128)}, u32[]{:S(2)}) copy-start(s32[1,1,80]{2,1,0:T(1,128)} %param.18) | copy-start | bytes 964
  22.9 2.3 %collective-permute-start.11 = (f32[1536,128]{1,0:T(8,128)S(1)}, f32[1536,128]{1,0:T(8,128)S(1)}, u32[]{:S(2)}, u32[]{:S(2)}) collective-permute-start(f32[1536,128]{1,0:T(8,128)S(1)} %collective-permute-done.10.refs_2_), channel_id=1, source_target_pairs={{0,1},{1,0},{2,3},{3,2},{4,5},{5,4},{6,7},{7,6},{8,9},{9,8},{10,11... | collective-permute-start | bytes 2359304 | tf_op jit(solution)/shard_map/ppermute | solution.py:20
  26.9 11.2 %collective-permute-start.3 = (f32[480,128]{1,0:T(8,128)S(1)}, f32[480,128]{1,0:T(8,128)S(1)}, u32[]{:S(2)}, u32[]{:S(2)}) collective-permute-start(f32[480,128]{1,0:T(8,128)S(1)} %get-tuple-element.74), channel_id=1, source_target_pairs={{0,28},{4,0},{8,4},{12,8},{16,12},{20,16},{24,20},{28,24},{1,29},{... | collective-permute-start | bytes 737288 | tf_op jit(solution)/shard_map/cond/branch_1_fun/ppermute | solution.py:25
  34.8 9.7 %collective-permute-start.4 = (f32[488,128]{1,0:T(8,128)S(1)}, f32[488,128]{1,0:T(8,128)}, u32[]{:S(2)}, u32[]{:S(2)}) collective-permute-start(f32[488,128]{1,0:T(8,128)S(1)} %branch_1_fun.3), channel_id=1, source_target_pairs={{0,4},{4,8},{8,12},{12,16},{16,20},{20,24},{24,28},{28,0},{1,5},{5... | collective-permute-start | bytes 749576 | tf_op jit(solution)/shard_map/cond/branch_1_fun/ppermute | solution.py:25
  44.6 29.2 %copy-start.3 = (f32[32768]{0:T(1024)S(1)}, f32[32768]{0:T(1024)}, u32[]{:S(2)}) copy-start(f32[32768]{0:T(1024)} %param.16) | copy-start | bytes 393220
  44.6 25.0 %collective-permute-start.20 = (f32[488,128]{1,0:T(8,128)}, f32[488,128]{1,0:T(8,128)S(1)}, u32[]{:S(2)}, u32[]{:S(2)}) collective-permute-start(f32[488,128]{1,0:T(8,128)} %get-tuple-element.120.refs_1_), channel_id=1, source_target_pairs={{0,2},{1,3},{2,0},{3,1},{4,6},{5,7},{6,4},{7,5},{8,10},{9,11},{10,... | collective-permute-start | bytes 749576 | tf_op jit(solution)/shard_map/ppermute | solution.py:20
  44.6 25.1 %collective-permute-start.19 = (f32[488,128]{1,0:T(8,128)S(1)}, f32[488,128]{1,0:T(8,128)S(1)}, u32[]{:S(2)}, u32[]{:S(2)}) collective-permute-start(f32[488,128]{1,0:T(8,128)S(1)} %get-tuple-element.119.refs_0_), channel_id=1, source_target_pairs={{0,2},{1,3},{2,0},{3,1},{4,6},{5,7},{6,4},{7,5},{8,10},{9,11},{10,... | collective-permute-start | bytes 749576 | tf_op jit(solution)/shard_map/ppermute | solution.py:20
  46.6 10.6 %collective-permute-start.12 = (f32[48,128]{1,0:T(8,128)S(1)}, f32[48,128]{1,0:T(8,128)S(1)}, u32[]{:S(2)}, u32[]{:S(2)}) collective-permute-start(f32[48,128]{1,0:T(8,128)S(1)} %get-tuple-element.118), channel_id=1, source_target_pairs={{0,2},{1,3},{2,0},{3,1},{4,6},{5,7},{6,4},{7,5},{8,10},{9,11},{10,... | collective-permute-start | bytes 73736 | tf_op jit(solution)/shard_map/ppermute | solution.py:20
  57.2 3.8 %collective-permute-start.13 = (f32[48,128]{1,0:T(8,128)S(1)}, f32[48,128]{1,0:T(8,128)S(1)}, u32[]{:S(2)}, u32[]{:S(2)}) collective-permute-start(f32[48,128]{1,0:T(8,128)S(1)} %add.31), channel_id=1, source_target_pairs={{0,4},{4,0},{8,12},{12,8},{16,20},{20,16},{24,28},{28,24},{1,5},{5... | collective-permute-start | bytes 73736 | tf_op jit(solution)/shard_map/ppermute | solution.py:20
  61.0 3.8 %collective-permute-start.14 = (f32[48,128]{1,0:T(8,128)S(1)}, f32[48,128]{1,0:T(8,128)S(1)}, u32[]{:S(2)}, u32[]{:S(2)}) collective-permute-start(f32[48,128]{1,0:T(8,128)S(1)} %add.32), channel_id=1, source_target_pairs={{0,8},{4,12},{8,0},{12,4},{16,24},{20,28},{24,16},{28,20},{1,9},{5... | collective-permute-start | bytes 73736 | tf_op jit(solution)/shard_map/ppermute | solution.py:20
  61.0 10.5 %collective-permute-start.17 = (f32[488,128]{1,0:T(8,128)S(1)}, f32[488,128]{1,0:T(8,128)S(1)}, u32[]{:S(2)}, u32[]{:S(2)}) collective-permute-start(f32[488,128]{1,0:T(8,128)S(1)} %get-tuple-element.119.refs_0_), channel_id=1, source_target_pairs={{0,1},{1,0},{2,3},{3,2},{4,5},{5,4},{6,7},{7,6},{8,9},{9,8},{10,11... | collective-permute-start | bytes 749576 | tf_op jit(solution)/shard_map/ppermute | solution.py:20
  61.1 10.5 %collective-permute-start.18 = (f32[488,128]{1,0:T(8,128)}, f32[488,128]{1,0:T(8,128)S(1)}, u32[]{:S(2)}, u32[]{:S(2)}) collective-permute-start(f32[488,128]{1,0:T(8,128)} %get-tuple-element.120.refs_1_), channel_id=1, source_target_pairs={{0,1},{1,0},{2,3},{3,2},{4,5},{5,4},{6,7},{7,6},{8,9},{9,8},{10,11... | collective-permute-start | bytes 749576 | tf_op jit(solution)/shard_map/ppermute | solution.py:20
  64.9 4.7 %collective-permute-start.15 = (f32[48,128]{1,0:T(8,128)S(1)}, f32[48,128]{1,0:T(8,128)S(1)}, u32[]{:S(2)}, u32[]{:S(2)}) collective-permute-start(f32[48,128]{1,0:T(8,128)S(1)} %add.33), channel_id=1, source_target_pairs={{0,16},{4,20},{8,24},{12,28},{16,0},{20,4},{24,8},{28,12},{1,17},{... | collective-permute-start | bytes 73736 | tf_op jit(solution)/shard_map/ppermute | solution.py:20
  69.6 3.5 %collective-permute-start.22 = (f32[488,128]{1,0:T(8,128)S(1)}, f32[488,128]{1,0:T(8,128)S(1)}, u32[]{:S(2)}, u32[]{:S(2)}) collective-permute-start(f32[488,128]{1,0:T(8,128)S(1)} %collective-permute-done.20.refs_2_), channel_id=1, source_target_pairs={{0,1},{1,0},{2,3},{3,2},{4,5},{5,4},{6,7},{7,6},{8,9},{9,8},{10,11... | collective-permute-start | bytes 749576 | tf_op jit(solution)/shard_map/ppermute | solution.py:20
  69.7 3.4 %collective-permute-start.21 = (f32[488,128]{1,0:T(8,128)S(1)}, f32[488,128]{1,0:T(8,128)S(1)}, u32[]{:S(2)}, u32[]{:S(2)}) collective-permute-start(f32[488,128]{1,0:T(8,128)S(1)} %collective-permute-done.19.refs_1_), channel_id=1, source_target_pairs={{0,1},{1,0},{2,3},{3,2},{4,5},{5,4},{6,7},{7,6},{8,9},{9,8},{10,11... | collective-permute-start | bytes 749576 | tf_op jit(solution)/shard_map/ppermute | solution.py:20
  70.2 1.4 %collective-permute-start.16 = (f32[48,128]{1,0:T(8,128)S(1)}, f32[48,128]{1,0:T(8,128)S(1)}, u32[]{:S(2)}, u32[]{:S(2)}) collective-permute-start(f32[48,128]{1,0:T(8,128)S(1)} %add.34), channel_id=1, source_target_pairs={{0,1},{1,0},{2,3},{3,2},{4,5},{5,4},{6,7},{7,6},{8,9},{9,8},{10,11... | collective-permute-start | bytes 73736 | tf_op jit(solution)/shard_map/ppermute | solution.py:20
where the time goes:
time: 76.9 us; the launch traced here: 76.7 us
  waiting for transfers between devices  39.2 us (51%)
  Pallas kernels  16.6 us (22%)
  starting transfers between devices  12.7 us (17%)
  local copies, waits for them, and re-layouts  5.22 us (7%)
  between operations  2.11 us (3%)
    ppermute x14, waiting for transfers between devices, swap(): return lax.ppermute(x, axis, [(i, i ^ mask) for i in range(n)])  29.3 us
    pallas_call x9, Pallas kernels, call(): pl.pallas_call(kernel, out_shape=out_shape, in_specs=in_specs or [VMEM] *...  16.6 us
    ppermute x3, waiting for transfers between devices, shift(): return lax.ppermute(x, 'row', [(i, (i + distance) % n) for i in range(n)])  9.88 us
    ppermute x3, starting transfers between devices, shift(): return lax.ppermute(x, 'row', [(i, (i + distance) % n) for i in range(n)])  6.37 us
    ppermute x14, starting transfers between devices, swap(): return lax.ppermute(x, axis, [(i, i ^ mask) for i in range(n)])  6.34 us
    unnamed x14, local copies, waits for them, and re-layouts  4.62 us
  transfers between devices with their start and end apart: 17, of which 10 were waited for; matrix products, arithmetic and copies ran while one was open for 2% of the time, Pallas kernels for 14%

commit v1 on v0

--- a/solution.py
+++ b/solution.py
@@ -138,7 +138,7 @@
         low = jnp.concatenate([lo, jnp.zeros_like(lo)], axis=1)
         return [top, low]
 
-    @pl.loop(0, step // 2, unroll=2)
+    @pl.loop(0, step // 2, unroll=step // 2)
     def _(p):
         i = 2 * p
         x = jnp.concatenate(left(base + i) + left(base + i + 1), axis=0).astype(BF16)
@@ -164,23 +164,23 @@
 
             @pl.when(pl.program_id(0) == pl.num_programs(0) - 1)
             def _():
-                couple(vectors, slots, refs[0], o_ref, refs[1], refs[3])
-                refs[4][...] = refs[3][...]
+                couple(vectors, slots, refs[0], o_ref, refs[1], refs[3], refs[4])
 
     out = jax.ShapeDtypeStruct((rows + 8, width), F32)
     if coupled:
-        sums = jax.ShapeDtypeStruct((-(-2 * count // 8) * 8, width), F32)
-        out = (out, sums, sums)
+        out = (out, jax.ShapeDtypeStruct((8, width), F32))
     operands = (x, high, low, ids) + (coupled or ())
     return call(
         kernel, out, operands, [VMEM, spec, spec] + [VMEM] * (len(operands) - 3), 12,
         flops=slots * 2 * 32 * 256 * 128, grid=(slots // step,),
-    )
-
-
-def couple(vectors, slots, x_ref, y_ref, p_ref, o_ref):
+        scratch=(pltpu.VMEM((-(-2 * count // 8) * 8, width), F32),) if coupled else (),
+    )
+
+
+def couple(vectors, slots, x_ref, y_ref, p_ref, o_ref, l_ref):
     both = pairs(vectors)
     n = len(both)
+    lines, width = l_ref.shape
 
     def step(c, sums):
         at = pl.multiple_of(8 * c * vectors, 8)
@@ -192,11 +192,15 @@
     sums = lax.fori_loop(0, slots // 8, step, sums)
     sums = [p_ref[pl.ds(8 * k, 8), :] for k in range(n)] + list(sums)
     for k, s in enumerate(sums):
-        o_ref[k : k + 1, :] = jnp.sum(s, axis=0, keepdims=True)
-    if o_ref.shape[0] > 2 * n:
-        o_ref[2 * n :, :] = jnp.zeros((o_ref.shape[0] - 2 * n, o_ref.shape[1]), F32)
-    total = jnp.sum(o_ref[...], axis=1, keepdims=True)
-    o_ref[...] = jnp.broadcast_to(total, o_ref.shape)
+        l_ref[k : k + 1, :] = jnp.sum(s, axis=0, keepdims=True)
+    if lines > 2 * n:
+        l_ref[2 * n :, :] = jnp.zeros((lines - 2 * n, width), F32)
+    lane = lax.broadcasted_iota(jnp.int32, (8, width), 1)
+    tile = jnp.zeros((8, width), F32)
+    for g in range(lines // 8):
+        part = jnp.sum(l_ref[pl.ds(8 * g, 8), :], axis=1, keepdims=True)
+        tile = jnp.where(lane == g, part, tile)
+    o_ref[...] = tile
 
 
 def add_kernel(vectors, slots, blocks, started, me_ref, *refs):
@@ -277,7 +281,7 @@
     return inv, onto
 
 
-def finish_kernel(vectors, total, steps, sums_ref, x_ref, d_ref, m_ref, final_ref, residual_ref, coef, res, fin):
+def finish_kernel(vectors, total, steps, tile_ref, x_ref, d_ref, m_ref, final_ref, residual_ref, coef, res, fin, sums_ref):
     blocks, width = d_ref.shape
     chunk = blocks // steps
     start = pl.program_id(0) * chunk
@@ -289,12 +293,14 @@
 
     @pl.when(pl.program_id(0) == 0)
     def _():
+        for g in range(sums_ref.shape[0] // 8):
+            sums_ref[pl.ds(8 * g, 8), :] = jnp.broadcast_to(tile_ref[:, g : g + 1], (8, width))
         inv, onto = algebra(vectors, total, sums_ref)
         for name, table in (("i", inv), ("o", onto)):
             for key in table:
                 coef[pl.ds(8 * places[name, key], 8), :] = jnp.broadcast_to(table[key], (8, width))
 
-    @pl.loop(0, chunk // 8, unroll=2)
+    @pl.loop(0, chunk // 8, unroll=4)
     def _(c):
         local = pl.multiple_of(c * 8, 8)
         at = pl.multiple_of(start + local, 8)
@@ -378,7 +384,7 @@
         arrived = shift(picked_col, -s) if s else picked_col
         mirrored = multiply(picked_row, high, low, col_line, vectors, False)
         returned = shift(mirrored, s) if s else mirrored
-        direct, sums, _ = multiply(arrived, high, low, row_line, vectors, True, (picked_row, inner))
+        direct, sums = multiply(arrived, high, low, row_line, vectors, True, (picked_row, inner))
         return direct, returned, sums
 
     direct, returned, sums = lax.switch(
@@ -398,7 +404,7 @@
     sums = sum_step(stages[-1], *order[-1])
     image = add_lists(me[None], lists[half:], vectors, slots, blocks, image)
     out = jax.ShapeDtypeStruct((vectors, shard), F32)
-    steps = 4 if blocks % 64 == 0 else 1
+    steps = 2 if blocks % 64 == 0 else 1
     spec = pl.BlockSpec((vectors, shard // steps), lambda i: (0, i))
     return call(
         functools.partial(finish_kernel, vectors, float(total), steps), (out, out),
@@ -407,6 +413,7 @@
             pltpu.VMEM((8 * (vectors * vectors + count), width), F32),
             pltpu.VMEM((8 * blocks // steps, width), F32),
             pltpu.VMEM((8 * blocks // steps, width), F32),
+            pltpu.VMEM((-(-2 * count // 8) * 8, width), F32),
         ),
         grid=(steps,), out_specs=(spec, spec),
     )

time: 76.9 us -> 73.7 us (0.958)
  Pallas kernels: 16.6 us -> 12.1 us
  starting transfers between devices: 12.7 us -> 13.8 us
    pallas_call x9, Pallas kernels: 16.6 us -> 12.1 us  [call(): pl.pallas_call(kernel, out_shape=out_shape, in_specs=in_specs or [VMEM] *...]
    ppermute x3, waiting for transfers between devices: 9.88 us -> 12.3 us  [shift(): return lax.ppermute(x, 'row', [(i, (i + distance) % n) for i in range(n)])]
    ppermute x14, waiting for transfers between devices: 29.3 us -> 27 us  [swap(): return lax.ppermute(x, axis, [(i, i ^ mask) for i in range(n)])]
    ppermute x14, starting transfers between devices: 6.34 us -> 7.43 us  [swap(): return lax.ppermute(x, axis, [(i, i ^ mask) for i in range(n)])]
  transfers between devices with their start and end apart: 17 -> 17, of which waited for: 10 -> 10; matrix products, arithmetic and copies ran while one was open for 2% -> 2% of each run, Pallas kernels for 14% -> 9%
where the time goes in v1:
time: 73.7 us; the launch traced here: 73.4 us
  waiting for transfers between devices  39.4 us (53%)
  starting transfers between devices  13.8 us (19%)
  Pallas kernels  12.1 us (16%)
  local copies, waits for them, and re-layouts  5.22 us (7%)
  between operations  2.09 us (3%)
    ppermute x14, waiting for transfers between devices, swap(): return lax.ppermute(x, axis, [(i, i ^ mask) for i in range(n)])  27 us
    ppermute x3, waiting for transfers between devices, shift(): return lax.ppermute(x, 'row', [(i, (i + distance) % n) for i in range(n)])  12.3 us
    pallas_call x9, Pallas kernels, call(): pl.pallas_call(kernel, out_shape=out_shape, in_specs=in_specs or [VMEM] *...  12.1 us
    ppermute x14, starting transfers between devices, swap(): return lax.ppermute(x, axis, [(i, i ^ mask) for i in range(n)])  7.43 us
    ppermute x3, starting transfers between devices, shift(): return lax.ppermute(x, 'row', [(i, (i + distance) % n) for i in range(n)])  6.41 us
    unnamed x14, local copies, waits for them, and re-layouts  4.62 us
  transfers between devices with their start and end apart: 17, of which 10 were waited for; matrix products, arithmetic and copies ran while one was open for 2% of the time, Pallas kernels for 9%

profile of v1, /device:TPU:0, one launch (start us, length us, event | category | flops | bytes accessed | tf_op | source)
XLA Modules:
  0.0 73.4 jit_solution(3338037756331885660)
XLA Ops:
  0.6 1.2 %copy-done.1 = f32[6,32768]{1,0:T(8,128)S(1)} copy-done((f32[6,32768]{1,0:T(8,128)S(1)}, f32[6,32768]{1,0:T(8,128)}, u32[]{:S(2)}) %copy-start.1) | copy-done | bytes 786456
  2.3 3.1 %collective-permute-start.10 = (f32[1536,128]{1,0:T(8,128)S(1)}, f32[1536,128]{1,0:T(8,128)S(1)}, u32[]{:S(2)}, u32[]{:S(2)}) collective-permute-start(f32[1536,128]{1,0:T(8,128)S(1)} %shard_map.86.x_ref.refs_0_), channel_id=1, source_target_pairs={{0,2},{1,3},{2,0},{3,1},{4,6},{5,7},{6,4},{7,5},{8,10},{9,11},{10,... | collective-permute-start | bytes 2359304 | tf_op jit(solution)/shard_map/ppermute | solution.py:20
  6.0 0.9 %copy-done.2 = f32[32768]{0:T(1024)S(1)} copy-done((f32[32768]{0:T(1024)S(1)}, f32[32768]{0:T(1024)}, u32[]{:S(2)}) %copy-start.2) | copy-done | bytes 131096
  6.9 0.8 %shard_map.87 = f32[336,128]{1,0:T(8,128)S(1)} custom-call(f32[1536,128]{1,0:T(8,128)S(1)} %shard_map.86.x_ref.refs_0_, f32[256,128]{1,0:T(8,128)S(1)} %bitcast.13), custom_call_target="tpu_custom_call" | custom-call | bytes 917504 | tf_op jit(solution)/shard_map/pallas_call | solution.py:56
  7.7 0.6 dynamic_slice.3
  9.0 6.5 %conditional.2 = (f32[8,128]{1,0:T(8,128)}) conditional(s32[]{:T(128)} %bitcast, f32[8,128]{1,0:T(8,128)S(1)} %pad.9, f32[8,128]{1,0:T(8,128)S(1)} %pad.9, f32[8,128]{1,0:T(8,128)S(1)} %pad.9, f32[8,128]{1,0:T(8,128)S(1)} %pad.9), branch_computations={%region_0.1_spmd, %region_1.2_spmd, %region_2.3_spmd, %region_3.4_... | conditional | bytes 16432 | solution.py:359
  9.0 1.5 %collective-permute-start = (f32[8,128]{1,0:T(8,128)S(1)}, f32[8,128]{1,0:T(8,128)}, u32[]{:S(2)}, u32[]{:S(2)}) collective-permute-start(f32[8,128]{1,0:T(8,128)S(1)} %param.1), channel_id=1, source_target_pairs={{0,4},{4,8},{8,12},{12,16},{16,20},{20,24},{24,28},{28,0},{1,5},{5... | collective-permute-start | bytes 12296 | tf_op jit(solution)/shard_map/cond/branch_1_fun/ppermute | solution.py:25
  10.5 4.9 %collective-permute-done = f32[8,128]{1,0:T(8,128)} collective-permute-done((f32[8,128]{1,0:T(8,128)S(1)}, f32[8,128]{1,0:T(8,128)}, u32[]{:S(2)}, u32[]{:S(2)}) %collective-permute-start) | collective-permute-done | bytes 4128 | tf_op jit(solution)/shard_map/cond/branch_1_fun/ppermute | solution.py:25
  15.5 2.5 %copy-done = f32[1,1,80,128,128]{4,3,2,1,0:T(8,128)S(1)} copy-done((f32[1,1,80,128,128]{4,3,2,1,0:T(8,128)S(1)}, f32[1,1,80,128,128]{4,3,2,1,0:T(8,128)}, u32[]{:S(2)}) %copy-start) | copy-done | bytes 5242904
  17.9 0.9 %shard_map.88 = (bf16[80,128,128]{2,1,0:T(8,128)(2,1)S(1)}, bf16[80,128,128]{2,1,0:T(8,128)(2,1)S(1)}) custom-call(f32[80,128,128]{2,1,0:T(8,128)S(1)} %bitcast.12), custom_call_target="tpu_custom_call" | custom-call | flops 5242880 | bytes 5242880 | tf_op jit(solution)/shard_map/pallas_call | solution.py:56
  18.9 0.7 slice_convert_fusion
  19.6 3.3 %collective-permute-done.10.refs_2_ = f32[1536,128]{1,0:T(8,128)S(1)} collective-permute-done((f32[1536,128]{1,0:T(8,128)S(1)}, f32[1536,128]{1,0:T(8,128)S(1)}, u32[]{:S(2)}, u32[]{:S(2)}) %collective-permute-start.10) | collective-permute-done | bytes 786464 | tf_op jit(solution)/shard_map/ppermute | solution.py:20
  22.9 2.3 %collective-permute-done.11.refs_3_ = f32[1536,128]{1,0:T(8,128)S(1)} collective-permute-done((f32[1536,128]{1,0:T(8,128)S(1)}, f32[1536,128]{1,0:T(8,128)S(1)}, u32[]{:S(2)}, u32[]{:S(2)}) %collective-permute-start.11) | collective-permute-done | bytes 786464 | tf_op jit(solution)/shard_map/ppermute | solution.py:20
  25.2 1.7 %shard_map.89 = (f32[480,128]{1,0:T(8,128)S(1)}, f32[480,128]{1,0:T(8,128)S(1)}) custom-call(s32[2,80]{1,0:T(2,128)S(1)} %get-tuple-element.126.where_ref, s32[2,80]{1,0:T(2,128)S(1)} %get-tuple-element.125.at_ref, f32[1536,128]{1,0:T(8,128)S(1)} %shard_map.86.x_ref.refs_0_, f32[1536,128]{1,0:T(8,128)S(1)} %collective-permute-done.9.refs_1_, ...), custom_call_target="tpu_custom_call" | custom-call | bytes 3147008 | tf_op jit(solution)/shard_map/pallas_call | solution.py:56
  26.9 15.9 %conditional.3 = (f32[488,128]{1,0:T(8,128)S(1)}, f32[488,128]{1,0:T(8,128)}, f32[8,128]{1,0:T(8,128)S(1)}) conditional(s32[]{:T(128)} %bitcast, (f32[480,128]{1,0:T(8,128)S(1)}, bf16[80,128,128]{2,1,0:T(8,128)(2,1)S(1)}, bf16[80,128,128]{2,1,0:T(8,128)(2,1)S(1)}, f32[8,128]{1,0:T(8,128)S(1)}, ...), branch_computations={%region_4.5_spmd, %region_5.6_spmd, %region_6.7_spmd, %region_7.8_... | conditional | flops 335544320 | bytes 13385832 | solution.py:390
  26.9 4.8 %collective-permute-start.3 = (f32[480,128]{1,0:T(8,128)S(1)}, f32[480,128]{1,0:T(8,128)S(1)}, u32[]{:S(2)}, u32[]{:S(2)}) collective-permute-start(f32[480,128]{1,0:T(8,128)S(1)} %get-tuple-element.74), channel_id=1, source_target_pairs={{0,28},{4,0},{8,4},{12,8},{16,12},{20,16},{24,20},{28,24},{1,29},{... | collective-permute-start | bytes 737288 | tf_op jit(solution)/shard_map/cond/branch_1_fun/ppermute | solution.py:25
  31.7 1.3 %branch_1_fun.3 = f32[488,128]{1,0:T(8,128)S(1)} custom-call(f32[480,128]{1,0:T(8,128)S(1)} %get-tuple-element.78.refs_0_.x_ref, bf16[80,128,128]{2,1,0:T(8,128)(2,1)S(1)} %get-tuple-element.75.hi_ref, bf16[80,128,128]{2,1,0:T(8,128)(2,1)S(1)} %get-tuple-element.76.lo_ref, f32[8,128]{1,0:T(8,128)S(1)} %get-tuple-element.81.ids_ref), custom_call_target="tpu_custom_call" | custom-call | flops 167772160 | bytes 5492736 | tf_op jit(solution)/shard_map/cond/branch_1_fun/pallas_call | solution.py:56
  33.1 5.0 %collective-permute-done.3.x_ref = f32[480,128]{1,0:T(8,128)S(1)} collective-permute-done((f32[480,128]{1,0:T(8,128)S(1)}, f32[480,128]{1,0:T(8,128)S(1)}, u32[]{:S(2)}, u32[]{:S(2)}) %collective-permute-start.3) | collective-permute-done | bytes 245792 | tf_op jit(solution)/shard_map/cond/branch_1_fun/ppermute | solution.py:25
  38.1 2.3 %branch_1_fun.2 = (f32[488,128]{1,0:T(8,128)S(1)}, f32[8,128]{1,0:T(8,128)S(1)}) custom-call(f32[480,128]{1,0:T(8,128)S(1)} %collective-permute-done.3.x_ref, bf16[80,128,128]{2,1,0:T(8,128)(2,1)S(1)} %get-tuple-element.75.hi_ref, bf16[80,128,128]{2,1,0:T(8,128)(2,1)S(1)} %get-tuple-element.76.lo_ref, f32[8,128]{1,0:T(8,128)S(1)} %get-tuple-element.77.ids_ref, ...), custom_call_target="tpu_custom_call" | custom-call | flops 167772160 | bytes 5910528 | tf_op jit(solution)/shard_map/cond/branch_1_fun/pallas_call | solution.py:56
  40.4 2.4 %collective-permute-done.4 = f32[488,128]{1,0:T(8,128)} collective-permute-done((f32[488,128]{1,0:T(8,128)S(1)}, f32[488,128]{1,0:T(8,128)}, u32[]{:S(2)}, u32[]{:S(2)}) %collective-permute-start.4) | collective-permute-done | bytes 249888 | tf_op jit(solution)/shard_map/cond/branch_1_fun/ppermute | solution.py:25
  42.8 2.0 %collective-permute-start.19 = (f32[488,128]{1,0:T(8,128)S(1)}, f32[488,128]{1,0:T(8,128)S(1)}, u32[]{:S(2)}, u32[]{:S(2)}) collective-permute-start(f32[488,128]{1,0:T(8,128)S(1)} %get-tuple-element.119.refs_0_), channel_id=1, source_target_pairs={{0,2},{1,3},{2,0},{3,1},{4,6},{5,7},{6,4},{7,5},{8,10},{9,11},{10,... | collective-permute-start | bytes 749576 | tf_op jit(solution)/shard_map/ppermute | solution.py:20
  44.8 0.5 collective-permute-start.18
  45.4 9.6 %collective-permute-done.12 = f32[8,128]{1,0:T(8,128)S(1)} collective-permute-done((f32[8,128]{1,0:T(8,128)S(1)}, f32[8,128]{1,0:T(8,128)S(1)}, u32[]{:S(2)}, u32[]{:S(2)}) %collective-permute-start.12) | collective-permute-done | bytes 4128 | tf_op jit(solution)/shard_map/ppermute | solution.py:20
  55.0 3.6 %collective-permute-done.13 = f32[8,128]{1,0:T(8,128)S(1)} collective-permute-done((f32[8,128]{1,0:T(8,128)S(1)}, f32[8,128]{1,0:T(8,128)S(1)}, u32[]{:S(2)}, u32[]{:S(2)}) %collective-permute-start.13) | collective-permute-done | bytes 4128 | tf_op jit(solution)/shard_map/ppermute | solution.py:20
  58.8 3.4 %collective-permute-done.14 = f32[8,128]{1,0:T(8,128)S(1)} collective-permute-done((f32[8,128]{1,0:T(8,128)S(1)}, f32[8,128]{1,0:T(8,128)S(1)}, u32[]{:S(2)}, u32[]{:S(2)}) %collective-permute-start.14) | collective-permute-done | bytes 4128 | tf_op jit(solution)/shard_map/ppermute | solution.py:20
  62.2 1.1 %collective-permute-start.15 = (f32[8,128]{1,0:T(8,128)S(1)}, f32[8,128]{1,0:T(8,128)S(1)}, u32[]{:S(2)}, u32[]{:S(2)}) collective-permute-start(f32[8,128]{1,0:T(8,128)S(1)} %add.33), channel_id=1, source_target_pairs={{0,16},{4,20},{8,24},{12,28},{16,0},{20,4},{24,8},{28,12},{1,17},{... | collective-permute-start | bytes 12296 | tf_op jit(solution)/shard_map/ppermute | solution.py:20
  63.3 3.4 %collective-permute-done.15 = f32[8,128]{1,0:T(8,128)S(1)} collective-permute-done((f32[8,128]{1,0:T(8,128)S(1)}, f32[8,128]{1,0:T(8,128)S(1)}, u32[]{:S(2)}, u32[]{:S(2)}) %collective-permute-start.15) | collective-permute-done | bytes 4128 | tf_op jit(solution)/shard_map/ppermute | solution.py:20
  66.8 0.5 collective-permute-start.21
  67.3 1.3 %collective-permute-done.16 = f32[8,128]{1,0:T(8,128)S(1)} collective-permute-done((f32[8,128]{1,0:T(8,128)S(1)}, f32[8,128]{1,0:T(8,128)S(1)}, u32[]{:S(2)}, u32[]{:S(2)}) %collective-permute-start.16) | collective-permute-done | bytes 4128 | tf_op jit(solution)/shard_map/ppermute | solution.py:20
  68.6 1.5 %shard_map.90.refs_0_ = f32[1536,128]{1,0:T(8,128)S(1)} custom-call(s32[1]{0:T(128)} %bitcast.6.me_ref, f32[488,128]{1,0:T(8,128)S(1)} %get-tuple-element.119.refs_0_, f32[488,128]{1,0:T(8,128)} %get-tuple-element.120.refs_1_, f32[488,128]{1,0:T(8,128)S(1)} %collective-permute-done.17.refs_2_, f32[488,128]{1,0:T(8,128)S(1)} %collective-permute-done.18.refs_3_), custom_call_target="tpu_custom_call" | custom-call | flops 402653184 | bytes 999428 | tf_op jit(solution)/shard_map/pallas_call | solution.py:56
  70.2 0.6 shard_map.91.m_ref
  70.8 2.6 %shard_map.92 = (f32[6,32768]{1,0:T(8,128)}, f32[6,32768]{1,0:T(8,128)}) custom-call(f32[8,128]{1,0:T(8,128)S(1)} %add.35.tile_ref, f32[1536,128]{1,0:T(8,128)S(1)} %shard_map.86.x_ref.refs_0_, f32[256,128]{1,0:T(8,128)S(1)} %bitcast.14, f32[1536,128]{1,0:T(8,128)S(1)} %shard_map.91.m_ref), custom_call_target="tpu_custom_call" | custom-call | bytes 1708032 | tf_op jit(solution)/shard_map/pallas_call | solution.py:56
  (39 shorter events, 0.9 us)
Async XLA Ops:
  0.6 1.2 %copy-start.1 = (f32[6,32768]{1,0:T(8,128)S(1)}, f32[6,32768]{1,0:T(8,128)}, u32[]{:S(2)}) copy-start(f32[6,32768]{1,0:T(8,128)} %x_ref.1) | copy-start | bytes 2359300
  1.9 5.8 %copy-start.5 = (s32[4]{0:T(128)S(1)}, s32[4]{0:T(128)}, u32[]{:S(2)}) copy-start(s32[4]{0:T(128)} %param.21) | copy-start | bytes 52
  1.9 6.4 %copy-start.6 = (s32[1,1,80]{2,1,0:T(1,128)S(1)}, s32[1,1,80]{2,1,0:T(1,128)}, u32[]{:S(2)}) copy-start(s32[1,1,80]{2,1,0:T(1,128)} %param.19) | copy-start | bytes 964
  2.3 20.6 %collective-permute-start.10 = (f32[1536,128]{1,0:T(8,128)S(1)}, f32[1536,128]{1,0:T(8,128)S(1)}, u32[]{:S(2)}, u32[]{:S(2)}) collective-permute-start(f32[1536,128]{1,0:T(8,128)S(1)} %shard_map.86.x_ref.refs_0_), channel_id=1, source_target_pairs={{0,2},{1,3},{2,0},{3,1},{4,6},{5,7},{6,4},{7,5},{8,10},{9,11},{10,... | collective-permute-start | bytes 2359304 | tf_op jit(solution)/shard_map/ppermute | solution.py:20
  5.4 17.6 %collective-permute-start.9 = (f32[1536,128]{1,0:T(8,128)S(1)}, f32[1536,128]{1,0:T(8,128)S(1)}, u32[]{:S(2)}, u32[]{:S(2)}) collective-permute-start(f32[1536,128]{1,0:T(8,128)S(1)} %shard_map.86.x_ref.refs_0_), channel_id=1, source_target_pairs={{0,1},{1,0},{2,3},{3,2},{4,5},{5,4},{6,7},{7,6},{8,9},{9,8},{10,11... | collective-permute-start | bytes 2359304 | tf_op jit(solution)/shard_map/ppermute | solution.py:20
  6.0 0.9 %copy-start.2 = (f32[32768]{0:T(1024)S(1)}, f32[32768]{0:T(1024)}, u32[]{:S(2)}) copy-start(f32[32768]{0:T(1024)} %param.16) | copy-start | bytes 393220
  9.0 6.5 %collective-permute-start = (f32[8,128]{1,0:T(8,128)S(1)}, f32[8,128]{1,0:T(8,128)}, u32[]{:S(2)}, u32[]{:S(2)}) collective-permute-start(f32[8,128]{1,0:T(8,128)S(1)} %param.1), channel_id=1, source_target_pairs={{0,4},{4,8},{8,12},{12,16},{16,20},{20,24},{24,28},{28,0},{1,5},{5... | collective-permute-start | bytes 12296 | tf_op jit(solution)/shard_map/cond/branch_1_fun/ppermute | solution.py:25
  15.5 2.5 %copy-start = (f32[1,1,80,128,128]{4,3,2,1,0:T(8,128)S(1)}, f32[1,1,80,128,128]{4,3,2,1,0:T(8,128)}, u32[]{:S(2)}) copy-start(f32[1,1,80,128,128]{4,3,2,1,0:T(8,128)} %param.17) | copy-start | bytes 15728644
  17.9 0.9 %copy-start.4 = (s32[1,1,80]{2,1,0:T(1,128)S(1)}, s32[1,1,80]{2,1,0:T(1,128)}, u32[]{:S(2)}) copy-start(s32[1,1,80]{2,1,0:T(1,128)} %param.18) | copy-start | bytes 964
  22.9 2.3 %collective-permute-start.11 = (f32[1536,128]{1,0:T(8,128)S(1)}, f32[1536,128]{1,0:T(8,128)S(1)}, u32[]{:S(2)}, u32[]{:S(2)}) collective-permute-start(f32[1536,128]{1,0:T(8,128)S(1)} %collective-permute-done.10.refs_2_), channel_id=1, source_target_pairs={{0,1},{1,0},{2,3},{3,2},{4,5},{5,4},{6,7},{7,6},{8,9},{9,8},{10,11... | collective-permute-start | bytes 2359304 | tf_op jit(solution)/shard_map/ppermute | solution.py:20
  26.9 11.1 %collective-permute-start.3 = (f32[480,128]{1,0:T(8,128)S(1)}, f32[480,128]{1,0:T(8,128)S(1)}, u32[]{:S(2)}, u32[]{:S(2)}) collective-permute-start(f32[480,128]{1,0:T(8,128)S(1)} %get-tuple-element.74), channel_id=1, source_target_pairs={{0,28},{4,0},{8,4},{12,8},{16,12},{20,16},{24,20},{28,24},{1,29},{... | collective-permute-start | bytes 737288 | tf_op jit(solution)/shard_map/cond/branch_1_fun/ppermute | solution.py:25
  33.0 9.8 %collective-permute-start.4 = (f32[488,128]{1,0:T(8,128)S(1)}, f32[488,128]{1,0:T(8,128)}, u32[]{:S(2)}, u32[]{:S(2)}) collective-permute-start(f32[488,128]{1,0:T(8,128)S(1)} %branch_1_fun.3), channel_id=1, source_target_pairs={{0,4},{4,8},{8,12},{12,16},{16,20},{20,24},{24,28},{28,0},{1,5},{5... | collective-permute-start | bytes 749576 | tf_op jit(solution)/shard_map/cond/branch_1_fun/ppermute | solution.py:25
  42.8 28.0 %copy-start.3 = (f32[32768]{0:T(1024)S(1)}, f32[32768]{0:T(1024)}, u32[]{:S(2)}) copy-start(f32[32768]{0:T(1024)} %param.16) | copy-start | bytes 393220
  42.8 23.9 %collective-permute-start.20 = (f32[488,128]{1,0:T(8,128)}, f32[488,128]{1,0:T(8,128)S(1)}, u32[]{:S(2)}, u32[]{:S(2)}) collective-permute-start(f32[488,128]{1,0:T(8,128)} %get-tuple-element.120.refs_1_), channel_id=1, source_target_pairs={{0,2},{1,3},{2,0},{3,1},{4,6},{5,7},{6,4},{7,5},{8,10},{9,11},{10,... | collective-permute-start | bytes 749576 | tf_op jit(solution)/shard_map/ppermute | solution.py:20
  42.8 23.9 %collective-permute-start.19 = (f32[488,128]{1,0:T(8,128)S(1)}, f32[488,128]{1,0:T(8,128)S(1)}, u32[]{:S(2)}, u32[]{:S(2)}) collective-permute-start(f32[488,128]{1,0:T(8,128)S(1)} %get-tuple-element.119.refs_0_), channel_id=1, source_target_pairs={{0,2},{1,3},{2,0},{3,1},{4,6},{5,7},{6,4},{7,5},{8,10},{9,11},{10,... | collective-permute-start | bytes 749576 | tf_op jit(solution)/shard_map/ppermute | solution.py:20
  44.8 23.8 %collective-permute-start.17 = (f32[488,128]{1,0:T(8,128)S(1)}, f32[488,128]{1,0:T(8,128)S(1)}, u32[]{:S(2)}, u32[]{:S(2)}) collective-permute-start(f32[488,128]{1,0:T(8,128)S(1)} %get-tuple-element.119.refs_0_), channel_id=1, source_target_pairs={{0,1},{1,0},{2,3},{3,2},{4,5},{5,4},{6,7},{7,6},{8,9},{9,8},{10,11... | collective-permute-start | bytes 749576 | tf_op jit(solution)/shard_map/ppermute | solution.py:20
  44.8 23.8 %collective-permute-start.18 = (f32[488,128]{1,0:T(8,128)}, f32[488,128]{1,0:T(8,128)S(1)}, u32[]{:S(2)}, u32[]{:S(2)}) collective-permute-start(f32[488,128]{1,0:T(8,128)} %get-tuple-element.120.refs_1_), channel_id=1, source_target_pairs={{0,1},{1,0},{2,3},{3,2},{4,5},{5,4},{6,7},{7,6},{8,9},{9,8},{10,11... | collective-permute-start | bytes 749576 | tf_op jit(solution)/shard_map/ppermute | solution.py:20
  45.3 9.7 %collective-permute-start.12 = (f32[8,128]{1,0:T(8,128)S(1)}, f32[8,128]{1,0:T(8,128)S(1)}, u32[]{:S(2)}, u32[]{:S(2)}) collective-permute-start(f32[8,128]{1,0:T(8,128)S(1)} %get-tuple-element.118), channel_id=1, source_target_pairs={{0,2},{1,3},{2,0},{3,1},{4,6},{5,7},{6,4},{7,5},{8,10},{9,11},{10,... | collective-permute-start | bytes 12296 | tf_op jit(solution)/shard_map/ppermute | solution.py:20
  55.0 3.6 %collective-permute-start.13 = (f32[8,128]{1,0:T(8,128)S(1)}, f32[8,128]{1,0:T(8,128)S(1)}, u32[]{:S(2)}, u32[]{:S(2)}) collective-permute-start(f32[8,128]{1,0:T(8,128)S(1)} %add.31), channel_id=1, source_target_pairs={{0,4},{4,0},{8,12},{12,8},{16,20},{20,16},{24,28},{28,24},{1,5},{5... | collective-permute-start | bytes 12296 | tf_op jit(solution)/shard_map/ppermute | solution.py:20
  58.6 3.6 %collective-permute-start.14 = (f32[8,128]{1,0:T(8,128)S(1)}, f32[8,128]{1,0:T(8,128)S(1)}, u32[]{:S(2)}, u32[]{:S(2)}) collective-permute-start(f32[8,128]{1,0:T(8,128)S(1)} %add.32), channel_id=1, source_target_pairs={{0,8},{4,12},{8,0},{12,4},{16,24},{20,28},{24,16},{28,20},{1,9},{5... | collective-permute-start | bytes 12296 | tf_op jit(solution)/shard_map/ppermute | solution.py:20
  62.2 4.5 %collective-permute-start.15 = (f32[8,128]{1,0:T(8,128)S(1)}, f32[8,128]{1,0:T(8,128)S(1)}, u32[]{:S(2)}, u32[]{:S(2)}) collective-permute-start(f32[8,128]{1,0:T(8,128)S(1)} %add.33), channel_id=1, source_target_pairs={{0,16},{4,20},{8,24},{12,28},{16,0},{20,4},{24,8},{28,12},{1,17},{... | collective-permute-start | bytes 12296 | tf_op jit(solution)/shard_map/ppermute | solution.py:20
  66.7 3.4 %collective-permute-start.22 = (f32[488,128]{1,0:T(8,128)S(1)}, f32[488,128]{1,0:T(8,128)S(1)}, u32[]{:S(2)}, u32[]{:S(2)}) collective-permute-start(f32[488,128]{1,0:T(8,128)S(1)} %collective-permute-done.20.refs_2_), channel_id=1, source_target_pairs={{0,1},{1,0},{2,3},{3,2},{4,5},{5,4},{6,7},{7,6},{8,9},{9,8},{10,11... | collective-permute-start | bytes 749576 | tf_op jit(solution)/shard_map/ppermute | solution.py:20
  66.8 3.4 %collective-permute-start.21 = (f32[488,128]{1,0:T(8,128)S(1)}, f32[488,128]{1,0:T(8,128)S(1)}, u32[]{:S(2)}, u32[]{:S(2)}) collective-permute-start(f32[488,128]{1,0:T(8,128)S(1)} %collective-permute-done.19.refs_1_), channel_id=1, source_target_pairs={{0,1},{1,0},{2,3},{3,2},{4,5},{5,4},{6,7},{7,6},{8,9},{9,8},{10,11... | collective-permute-start | bytes 749576 | tf_op jit(solution)/shard_map/ppermute | solution.py:20
  67.2 1.4 %collective-permute-start.16 = (f32[8,128]{1,0:T(8,128)S(1)}, f32[8,128]{1,0:T(8,128)S(1)}, u32[]{:S(2)}, u32[]{:S(2)}) collective-permute-start(f32[8,128]{1,0:T(8,128)S(1)} %add.34), channel_id=1, source_target_pairs={{0,1},{1,0},{2,3},{3,2},{4,5},{5,4},{6,7},{7,6},{8,9},{9,8},{10,11... | collective-permute-start | bytes 12296 | tf_op jit(solution)/shard_map/ppermute | solution.py:20

commit v2 on v1

--- a/solution.py
+++ b/solution.py
@@ -114,7 +114,7 @@
     pieces, outs = refs[:-2], refs[-2:]
     for which, out in enumerate(outs):
 
-        @pl.loop(0, slots, unroll=4)
+        @pl.loop(0, slots, unroll=16 if slots % 16 == 0 else 1)
         def _(t):
             m = where_ref[which, t]
             at = at_ref[which, t]
@@ -300,7 +300,7 @@
             for key in table:
                 coef[pl.ds(8 * places[name, key], 8), :] = jnp.broadcast_to(table[key], (8, width))
 
-    @pl.loop(0, chunk // 8, unroll=4)
+    @pl.loop(0, chunk // 8, unroll=8 if chunk % 64 == 0 else 1)
     def _(c):
         local = pl.multiple_of(c * 8, 8)
         at = pl.multiple_of(start + local, 8)
@@ -323,7 +323,7 @@
             res[pl.ds(8 * local + i, 8, stride=8), :] = r
             fin[pl.ds(8 * local + i, 8, stride=8), :] = basis - r * rd
 
-    @pl.loop(0, chunk, unroll=8)
+    @pl.loop(0, chunk, unroll=16)
     def _(b):
         at = pl.multiple_of(b * width, width)
         residual_ref[:, pl.ds(at, width)] = res[pl.ds(pl.multiple_of(8 * b, 8), vectors), :]
@@ -356,11 +356,23 @@
         return jnp.pad(ids.astype(F32)[None, :], ((0, 7), (0, width - slots)), constant_values=-1)
 
     row_line, col_line = padded(row_ids), padded(col_ids)
-    group_line = lax.switch(
-        offset,
-        [functools.partial(lambda s, c: shift(c, s) if s else c, s) for s in distances],
-        col_line,
-    )
+
+    def routed(function, *operands):
+        if len(distances) <= 4:
+
+            def branch(s):
+                return functools.partial(function, lambda x, sign: shift(x, sign * s) if s else x)
+
+            return lax.switch(offset, [branch(s) for s in distances], *operands)
+
+        def move(x, sign):
+            for b in range((len(distances) - 1).bit_length()):
+                x = jnp.where(offset >> b & 1 == 1, shift(x, sign << b), x)
+            return x
+
+        return function(move, *operands)
+
+    group_line = routed(lambda move, line: move(line, 1), col_line)
     both = jnp.stack([row_ids, group_line[0, :slots].astype(jnp.int32)])
     where = jnp.where(both < 0, -1, (both // blocks) ^ me)
     at = jnp.where(both < 0, 0, both % blocks) * vectors
@@ -380,24 +392,22 @@
 
     row_bits, off_bits = bits_of("row")[::-1], bits_of("off")[::-1]
 
-    def middle(s, picked_row, picked_col, high, low, row_line, col_line, inner):
-        arrived = shift(picked_col, -s) if s else picked_col
+    def middle(move, picked_row, picked_col, high, low, row_line, col_line, inner):
+        arrived = move(picked_col, -1)
         mirrored = multiply(picked_row, high, low, col_line, vectors, False)
-        returned = shift(mirrored, s) if s else mirrored
+        returned = move(mirrored, 1)
         direct, sums = multiply(arrived, high, low, row_line, vectors, True, (picked_row, inner))
         return direct, returned, sums
 
-    direct, returned, sums = lax.switch(
-        offset,
-        [functools.partial(middle, s) for s in distances],
-        picked_row, picked_col, high, low, row_line, col_line, inner,
+    direct, returned, sums = routed(
+        middle, picked_row, picked_col, high, low, row_line, col_line, inner
     )
     stages = [sums]
     order = [("off", off_bits[-1])] + [("row", b) for b in row_bits] + [("off", b) for b in off_bits[:-1]]
     for axis, bit in order[:-1]:
         stages.append(sum_step(stages[-1], axis, bit))
     lists = []
-    for a, b in zip(gather_off(direct, (stages[-2],)), gather_off(returned, (stages[-1],))):
+    for a, b in zip(gather_off(direct, (stages[-2],)), gather_off(returned, (stages[-2],))):
         lists += [a, b]
     half = off_size
     image = add_lists(me[None], lists[:half], vectors, slots, blocks)

time: 73.7 us -> 73.2 us (level)
  no operation moved by 1% of the time
where the time goes in v2:
time: 73.2 us; the launch traced here: 72.9 us
  waiting for transfers between devices  39.2 us (54%)
  starting transfers between devices  13.8 us (19%)
  Pallas kernels  11.8 us (16%)
  local copies, waits for them, and re-layouts  5.22 us (7%)
  between operations  2.09 us (3%)
    ppermute x14, waiting for transfers between devices, swap(): return lax.ppermute(x, axis, [(i, i ^ mask) for i in range(n)])  26.9 us
    ppermute x3, waiting for transfers between devices, shift(): return lax.ppermute(x, 'row', [(i, (i + distance) % n) for i in range(n)])  12.3 us
    pallas_call x9, Pallas kernels, call(): pl.pallas_call(kernel, out_shape=out_shape, in_specs=in_specs or [VMEM] *...  11.8 us
    ppermute x14, starting transfers between devices, swap(): return lax.ppermute(x, axis, [(i, i ^ mask) for i in range(n)])  7.35 us
    ppermute x3, starting transfers between devices, shift(): return lax.ppermute(x, 'row', [(i, (i + distance) % n) for i in range(n)])  6.41 us
    unnamed x14, local copies, waits for them, and re-layouts  4.62 us
  transfers between devices with their start and end apart: 17, of which 10 were waited for; matrix products, arithmetic and copies ran while one was open for 2% of the time, Pallas kernels for 9%

profile of v2, /device:TPU:0, one launch (start us, length us, event | category | flops | bytes accessed | tf_op | source)
XLA Modules:
  0.0 72.9 jit_solution(3101747664918352296)
XLA Ops:
  0.6 1.2 %copy-done.1 = f32[6,32768]{1,0:T(8,128)S(1)} copy-done((f32[6,32768]{1,0:T(8,128)S(1)}, f32[6,32768]{1,0:T(8,128)}, u32[]{:S(2)}) %copy-start.1) | copy-done | bytes 786456
  2.3 3.1 %collective-permute-start.10 = (f32[1536,128]{1,0:T(8,128)S(1)}, f32[1536,128]{1,0:T(8,128)S(1)}, u32[]{:S(2)}, u32[]{:S(2)}) collective-permute-start(f32[1536,128]{1,0:T(8,128)S(1)} %shard_map.86.x_ref.refs_0_), channel_id=1, source_target_pairs={{0,2},{1,3},{2,0},{3,1},{4,6},{5,7},{6,4},{7,5},{8,10},{9,11},{10,... | collective-permute-start | bytes 2359304 | tf_op jit(solution)/shard_map/ppermute | solution.py:20
  6.0 0.9 %copy-done.2 = f32[32768]{0:T(1024)S(1)} copy-done((f32[32768]{0:T(1024)S(1)}, f32[32768]{0:T(1024)}, u32[]{:S(2)}) %copy-start.2) | copy-done | bytes 131096
  6.9 0.8 %shard_map.87 = f32[336,128]{1,0:T(8,128)S(1)} custom-call(f32[1536,128]{1,0:T(8,128)S(1)} %shard_map.86.x_ref.refs_0_, f32[256,128]{1,0:T(8,128)S(1)} %bitcast.13), custom_call_target="tpu_custom_call" | custom-call | bytes 917504 | tf_op jit(solution)/shard_map/pallas_call | solution.py:56
  7.7 0.6 dynamic_slice.3
  9.0 6.5 %conditional.2 = (f32[8,128]{1,0:T(8,128)}) conditional(s32[]{:T(128)} %bitcast, f32[8,128]{1,0:T(8,128)S(1)} %pad.9, f32[8,128]{1,0:T(8,128)S(1)} %pad.9, f32[8,128]{1,0:T(8,128)S(1)} %pad.9, f32[8,128]{1,0:T(8,128)S(1)} %pad.9), branch_computations={%region_0.1_spmd, %region_1.2_spmd, %region_2.3_spmd, %region_3.4_... | conditional | bytes 16432 | solution.py:366
  9.0 1.5 %collective-permute-start = (f32[8,128]{1,0:T(8,128)S(1)}, f32[8,128]{1,0:T(8,128)}, u32[]{:S(2)}, u32[]{:S(2)}) collective-permute-start(f32[8,128]{1,0:T(8,128)S(1)} %param.1), channel_id=1, source_target_pairs={{0,4},{4,8},{8,12},{12,16},{16,20},{20,24},{24,28},{28,0},{1,5},{5... | collective-permute-start | bytes 12296 | tf_op jit(solution)/shard_map/cond/branch_1_fun/ppermute | solution.py:25
  10.5 4.9 %collective-permute-done = f32[8,128]{1,0:T(8,128)} collective-permute-done((f32[8,128]{1,0:T(8,128)S(1)}, f32[8,128]{1,0:T(8,128)}, u32[]{:S(2)}, u32[]{:S(2)}) %collective-permute-start) | collective-permute-done | bytes 4128 | tf_op jit(solution)/shard_map/cond/branch_1_fun/ppermute | solution.py:25
  15.5 2.5 %copy-done = f32[1,1,80,128,128]{4,3,2,1,0:T(8,128)S(1)} copy-done((f32[1,1,80,128,128]{4,3,2,1,0:T(8,128)S(1)}, f32[1,1,80,128,128]{4,3,2,1,0:T(8,128)}, u32[]{:S(2)}) %copy-start) | copy-done | bytes 5242904
  17.9 0.9 %shard_map.88 = (bf16[80,128,128]{2,1,0:T(8,128)(2,1)S(1)}, bf16[80,128,128]{2,1,0:T(8,128)(2,1)S(1)}) custom-call(f32[80,128,128]{2,1,0:T(8,128)S(1)} %bitcast.12), custom_call_target="tpu_custom_call" | custom-call | flops 5242880 | bytes 5242880 | tf_op jit(solution)/shard_map/pallas_call | solution.py:56
  18.9 0.7 slice_convert_fusion
  19.6 3.3 %collective-permute-done.10.refs_2_ = f32[1536,128]{1,0:T(8,128)S(1)} collective-permute-done((f32[1536,128]{1,0:T(8,128)S(1)}, f32[1536,128]{1,0:T(8,128)S(1)}, u32[]{:S(2)}, u32[]{:S(2)}) %collective-permute-start.10) | collective-permute-done | bytes 786464 | tf_op jit(solution)/shard_map/ppermute | solution.py:20
  22.9 2.3 %collective-permute-done.11.refs_3_ = f32[1536,128]{1,0:T(8,128)S(1)} collective-permute-done((f32[1536,128]{1,0:T(8,128)S(1)}, f32[1536,128]{1,0:T(8,128)S(1)}, u32[]{:S(2)}, u32[]{:S(2)}) %collective-permute-start.11) | collective-permute-done | bytes 786464 | tf_op jit(solution)/shard_map/ppermute | solution.py:20
  25.2 1.5 %shard_map.89 = (f32[480,128]{1,0:T(8,128)S(1)}, f32[480,128]{1,0:T(8,128)S(1)}) custom-call(s32[2,80]{1,0:T(2,128)S(1)} %get-tuple-element.126.where_ref, s32[2,80]{1,0:T(2,128)S(1)} %get-tuple-element.125.at_ref, f32[1536,128]{1,0:T(8,128)S(1)} %shard_map.86.x_ref.refs_0_, f32[1536,128]{1,0:T(8,128)S(1)} %collective-permute-done.9.refs_1_, ...), custom_call_target="tpu_custom_call" | custom-call | bytes 3147008 | tf_op jit(solution)/shard_map/pallas_call | solution.py:56
  26.7 15.9 %conditional.3 = (f32[488,128]{1,0:T(8,128)S(1)}, f32[488,128]{1,0:T(8,128)}, f32[8,128]{1,0:T(8,128)S(1)}) conditional(s32[]{:T(128)} %bitcast, (f32[480,128]{1,0:T(8,128)S(1)}, bf16[80,128,128]{2,1,0:T(8,128)(2,1)S(1)}, bf16[80,128,128]{2,1,0:T(8,128)(2,1)S(1)}, f32[8,128]{1,0:T(8,128)S(1)}, ...), branch_computations={%region_4.5_spmd, %region_5.6_spmd, %region_6.7_spmd, %region_7.8_... | conditional | flops 335544320 | bytes 13385832 | solution.py:366
  26.8 4.8 %collective-permute-start.3 = (f32[480,128]{1,0:T(8,128)S(1)}, f32[480,128]{1,0:T(8,128)S(1)}, u32[]{:S(2)}, u32[]{:S(2)}) collective-permute-start(f32[480,128]{1,0:T(8,128)S(1)} %get-tuple-element.74), channel_id=1, source_target_pairs={{0,28},{4,0},{8,4},{12,8},{16,12},{20,16},{24,20},{28,24},{1,29},{... | collective-permute-start | bytes 737288 | tf_op jit(solution)/shard_map/cond/branch_1_fun/ppermute | solution.py:25
  31.6 1.3 %branch_1_fun.3 = f32[488,128]{1,0:T(8,128)S(1)} custom-call(f32[480,128]{1,0:T(8,128)S(1)} %get-tuple-element.78.refs_0_.x_ref, bf16[80,128,128]{2,1,0:T(8,128)(2,1)S(1)} %get-tuple-element.75.hi_ref, bf16[80,128,128]{2,1,0:T(8,128)(2,1)S(1)} %get-tuple-element.76.lo_ref, f32[8,128]{1,0:T(8,128)S(1)} %get-tuple-element.81.ids_ref), custom_call_target="tpu_custom_call" | custom-call | flops 167772160 | bytes 5492736 | tf_op jit(solution)/shard_map/cond/branch_1_fun/pallas_call | solution.py:56
  33.0 5.0 %collective-permute-done.3.x_ref = f32[480,128]{1,0:T(8,128)S(1)} collective-permute-done((f32[480,128]{1,0:T(8,128)S(1)}, f32[480,128]{1,0:T(8,128)S(1)}, u32[]{:S(2)}, u32[]{:S(2)}) %collective-permute-start.3) | collective-permute-done | bytes 245792 | tf_op jit(solution)/shard_map/cond/branch_1_fun/ppermute | solution.py:25
  37.9 2.3 %branch_1_fun.2 = (f32[488,128]{1,0:T(8,128)S(1)}, f32[8,128]{1,0:T(8,128)S(1)}) custom-call(f32[480,128]{1,0:T(8,128)S(1)} %collective-permute-done.3.x_ref, bf16[80,128,128]{2,1,0:T(8,128)(2,1)S(1)} %get-tuple-element.75.hi_ref, bf16[80,128,128]{2,1,0:T(8,128)(2,1)S(1)} %get-tuple-element.76.lo_ref, f32[8,128]{1,0:T(8,128)S(1)} %get-tuple-element.77.ids_ref, ...), custom_call_target="tpu_custom_call" | custom-call | flops 167772160 | bytes 5910528 | tf_op jit(solution)/shard_map/cond/branch_1_fun/pallas_call | solution.py:56
  40.2 2.4 %collective-permute-done.4 = f32[488,128]{1,0:T(8,128)} collective-permute-done((f32[488,128]{1,0:T(8,128)S(1)}, f32[488,128]{1,0:T(8,128)}, u32[]{:S(2)}, u32[]{:S(2)}) %collective-permute-start.4) | collective-permute-done | bytes 249888 | tf_op jit(solution)/shard_map/cond/branch_1_fun/ppermute | solution.py:25
  42.7 2.0 %collective-permute-start.19 = (f32[488,128]{1,0:T(8,128)S(1)}, f32[488,128]{1,0:T(8,128)S(1)}, u32[]{:S(2)}, u32[]{:S(2)}) collective-permute-start(f32[488,128]{1,0:T(8,128)S(1)} %get-tuple-element.119.refs_0_), channel_id=1, source_target_pairs={{0,2},{1,3},{2,0},{3,1},{4,6},{5,7},{6,4},{7,5},{8,10},{9,11},{10,... | collective-permute-start | bytes 749576 | tf_op jit(solution)/shard_map/ppermute | solution.py:20
  44.7 0.5 collective-permute-start.18
  45.2 9.6 %collective-permute-done.12 = f32[8,128]{1,0:T(8,128)S(1)} collective-permute-done((f32[8,128]{1,0:T(8,128)S(1)}, f32[8,128]{1,0:T(8,128)S(1)}, u32[]{:S(2)}, u32[]{:S(2)}) %collective-permute-start.12) | collective-permute-done | bytes 4128 | tf_op jit(solution)/shard_map/ppermute | solution.py:20
  54.9 3.6 %collective-permute-done.13 = f32[8,128]{1,0:T(8,128)S(1)} collective-permute-done((f32[8,128]{1,0:T(8,128)S(1)}, f32[8,128]{1,0:T(8,128)S(1)}, u32[]{:S(2)}, u32[]{:S(2)}) %collective-permute-start.13) | collective-permute-done | bytes 4128 | tf_op jit(solution)/shard_map/ppermute | solution.py:20
  58.6 3.5 %collective-permute-done.14 = f32[8,128]{1,0:T(8,128)S(1)} collective-permute-done((f32[8,128]{1,0:T(8,128)S(1)}, f32[8,128]{1,0:T(8,128)S(1)}, u32[]{:S(2)}, u32[]{:S(2)}) %collective-permute-start.14) | collective-permute-done | bytes 4128 | tf_op jit(solution)/shard_map/ppermute | solution.py:20
  62.1 0.5 collective-permute-start.21
  62.6 1.1 %collective-permute-start.15 = (f32[8,128]{1,0:T(8,128)S(1)}, f32[8,128]{1,0:T(8,128)S(1)}, u32[]{:S(2)}, u32[]{:S(2)}) collective-permute-start(f32[8,128]{1,0:T(8,128)S(1)} %add.33), channel_id=1, source_target_pairs={{0,16},{4,20},{8,24},{12,28},{16,0},{20,4},{24,8},{28,12},{1,17},{... | collective-permute-start | bytes 12296 | tf_op jit(solution)/shard_map/ppermute | solution.py:20
  63.7 3.4 %collective-permute-done.15 = f32[8,128]{1,0:T(8,128)S(1)} collective-permute-done((f32[8,128]{1,0:T(8,128)S(1)}, f32[8,128]{1,0:T(8,128)S(1)}, u32[]{:S(2)}, u32[]{:S(2)}) %collective-permute-start.15) | collective-permute-done | bytes 4128 | tf_op jit(solution)/shard_map/ppermute | solution.py:20
  67.1 1.2 %collective-permute-done.16 = f32[8,128]{1,0:T(8,128)S(1)} collective-permute-done((f32[8,128]{1,0:T(8,128)S(1)}, f32[8,128]{1,0:T(8,128)S(1)}, u32[]{:S(2)}, u32[]{:S(2)}) %collective-permute-start.16) | collective-permute-done | bytes 4128 | tf_op jit(solution)/shard_map/ppermute | solution.py:20
  68.3 1.5 %shard_map.90.refs_0_ = f32[1536,128]{1,0:T(8,128)S(1)} custom-call(s32[1]{0:T(128)} %bitcast.6.me_ref, f32[488,128]{1,0:T(8,128)S(1)} %get-tuple-element.119.refs_0_, f32[488,128]{1,0:T(8,128)} %get-tuple-element.120.refs_1_, f32[488,128]{1,0:T(8,128)S(1)} %collective-permute-done.17.refs_2_, f32[488,128]{1,0:T(8,128)S(1)} %collective-permute-done.18.refs_3_), custom_call_target="tpu_custom_call" | custom-call | flops 402653184 | bytes 999428 | tf_op jit(solution)/shard_map/pallas_call | solution.py:56
  69.8 0.6 shard_map.91.m_ref
  70.4 2.5 %shard_map.92 = (f32[6,32768]{1,0:T(8,128)}, f32[6,32768]{1,0:T(8,128)}) custom-call(f32[8,128]{1,0:T(8,128)S(1)} %add.35.tile_ref, f32[1536,128]{1,0:T(8,128)S(1)} %shard_map.86.x_ref.refs_0_, f32[256,128]{1,0:T(8,128)S(1)} %bitcast.14, f32[1536,128]{1,0:T(8,128)S(1)} %shard_map.91.m_ref), custom_call_target="tpu_custom_call" | custom-call | bytes 1708032 | tf_op jit(solution)/shard_map/pallas_call | solution.py:56
  (39 shorter events, 0.8 us)
Async XLA Ops:
  0.6 1.2 %copy-start.1 = (f32[6,32768]{1,0:T(8,128)S(1)}, f32[6,32768]{1,0:T(8,128)}, u32[]{:S(2)}) copy-start(f32[6,32768]{1,0:T(8,128)} %x_ref.1) | copy-start | bytes 2359300
  1.9 5.8 %copy-start.5 = (s32[4]{0:T(128)S(1)}, s32[4]{0:T(128)}, u32[]{:S(2)}) copy-start(s32[4]{0:T(128)} %param.21) | copy-start | bytes 52
  1.9 6.4 %copy-start.6 = (s32[1,1,80]{2,1,0:T(1,128)S(1)}, s32[1,1,80]{2,1,0:T(1,128)}, u32[]{:S(2)}) copy-start(s32[1,1,80]{2,1,0:T(1,128)} %param.19) | copy-start | bytes 964
  2.3 20.6 %collective-permute-start.10 = (f32[1536,128]{1,0:T(8,128)S(1)}, f32[1536,128]{1,0:T(8,128)S(1)}, u32[]{:S(2)}, u32[]{:S(2)}) collective-permute-start(f32[1536,128]{1,0:T(8,128)S(1)} %shard_map.86.x_ref.refs_0_), channel_id=1, source_target_pairs={{0,2},{1,3},{2,0},{3,1},{4,6},{5,7},{6,4},{7,5},{8,10},{9,11},{10,... | collective-permute-start | bytes 2359304 | tf_op jit(solution)/shard_map/ppermute | solution.py:20
  5.4 17.6 %collective-permute-start.9 = (f32[1536,128]{1,0:T(8,128)S(1)}, f32[1536,128]{1,0:T(8,128)S(1)}, u32[]{:S(2)}, u32[]{:S(2)}) collective-permute-start(f32[1536,128]{1,0:T(8,128)S(1)} %shard_map.86.x_ref.refs_0_), channel_id=1, source_target_pairs={{0,1},{1,0},{2,3},{3,2},{4,5},{5,4},{6,7},{7,6},{8,9},{9,8},{10,11... | collective-permute-start | bytes 2359304 | tf_op jit(solution)/shard_map/ppermute | solution.py:20
  6.0 0.9 %copy-start.2 = (f32[32768]{0:T(1024)S(1)}, f32[32768]{0:T(1024)}, u32[]{:S(2)}) copy-start(f32[32768]{0:T(1024)} %param.16) | copy-start | bytes 393220
  9.0 6.5 %collective-permute-start = (f32[8,128]{1,0:T(8,128)S(1)}, f32[8,128]{1,0:T(8,128)}, u32[]{:S(2)}, u32[]{:S(2)}) collective-permute-start(f32[8,128]{1,0:T(8,128)S(1)} %param.1), channel_id=1, source_target_pairs={{0,4},{4,8},{8,12},{12,16},{16,20},{20,24},{24,28},{28,0},{1,5},{5... | collective-permute-start | bytes 12296 | tf_op jit(solution)/shard_map/cond/branch_1_fun/ppermute | solution.py:25
  15.5 2.5 %copy-start = (f32[1,1,80,128,128]{4,3,2,1,0:T(8,128)S(1)}, f32[1,1,80,128,128]{4,3,2,1,0:T(8,128)}, u32[]{:S(2)}) copy-start(f32[1,1,80,128,128]{4,3,2,1,0:T(8,128)} %param.17) | copy-start | bytes 15728644
  17.9 0.9 %copy-start.4 = (s32[1,1,80]{2,1,0:T(1,128)S(1)}, s32[1,1,80]{2,1,0:T(1,128)}, u32[]{:S(2)}) copy-start(s32[1,1,80]{2,1,0:T(1,128)} %param.18) | copy-start | bytes 964
  22.9 2.3 %collective-permute-start.11 = (f32[1536,128]{1,0:T(8,128)S(1)}, f32[1536,128]{1,0:T(8,128)S(1)}, u32[]{:S(2)}, u32[]{:S(2)}) collective-permute-start(f32[1536,128]{1,0:T(8,128)S(1)} %collective-permute-done.10.refs_2_), channel_id=1, source_target_pairs={{0,1},{1,0},{2,3},{3,2},{4,5},{5,4},{6,7},{7,6},{8,9},{9,8},{10,11... | collective-permute-start | bytes 2359304 | tf_op jit(solution)/shard_map/ppermute | solution.py:20
  26.8 11.2 %collective-permute-start.3 = (f32[480,128]{1,0:T(8,128)S(1)}, f32[480,128]{1,0:T(8,128)S(1)}, u32[]{:S(2)}, u32[]{:S(2)}) collective-permute-start(f32[480,128]{1,0:T(8,128)S(1)} %get-tuple-element.74), channel_id=1, source_target_pairs={{0,28},{4,0},{8,4},{12,8},{16,12},{20,16},{24,20},{28,24},{1,29},{... | collective-permute-start | bytes 737288 | tf_op jit(solution)/shard_map/cond/branch_1_fun/ppermute | solution.py:25
  32.9 9.8 %collective-permute-start.4 = (f32[488,128]{1,0:T(8,128)S(1)}, f32[488,128]{1,0:T(8,128)}, u32[]{:S(2)}, u32[]{:S(2)}) collective-permute-start(f32[488,128]{1,0:T(8,128)S(1)} %branch_1_fun.3), channel_id=1, source_target_pairs={{0,4},{4,8},{8,12},{12,16},{16,20},{20,24},{24,28},{28,0},{1,5},{5... | collective-permute-start | bytes 749576 | tf_op jit(solution)/shard_map/cond/branch_1_fun/ppermute | solution.py:25
  42.7 27.8 %copy-start.3 = (f32[32768]{0:T(1024)S(1)}, f32[32768]{0:T(1024)}, u32[]{:S(2)}) copy-start(f32[32768]{0:T(1024)} %param.16) | copy-start | bytes 393220
  42.7 19.4 %collective-permute-start.20 = (f32[488,128]{1,0:T(8,128)}, f32[488,128]{1,0:T(8,128)S(1)}, u32[]{:S(2)}, u32[]{:S(2)}) collective-permute-start(f32[488,128]{1,0:T(8,128)} %get-tuple-element.120.refs_1_), channel_id=1, source_target_pairs={{0,2},{1,3},{2,0},{3,1},{4,6},{5,7},{6,4},{7,5},{8,10},{9,11},{10,... | collective-permute-start | bytes 749576 | tf_op jit(solution)/shard_map/ppermute | solution.py:20
  42.7 19.4 %collective-permute-start.19 = (f32[488,128]{1,0:T(8,128)S(1)}, f32[488,128]{1,0:T(8,128)S(1)}, u32[]{:S(2)}, u32[]{:S(2)}) collective-permute-start(f32[488,128]{1,0:T(8,128)S(1)} %get-tuple-element.119.refs_0_), channel_id=1, source_target_pairs={{0,2},{1,3},{2,0},{3,1},{4,6},{5,7},{6,4},{7,5},{8,10},{9,11},{10,... | collective-permute-start | bytes 749576 | tf_op jit(solution)/shard_map/ppermute | solution.py:20
  44.7 23.6 %collective-permute-start.17 = (f32[488,128]{1,0:T(8,128)S(1)}, f32[488,128]{1,0:T(8,128)S(1)}, u32[]{:S(2)}, u32[]{:S(2)}) collective-permute-start(f32[488,128]{1,0:T(8,128)S(1)} %get-tuple-element.119.refs_0_), channel_id=1, source_target_pairs={{0,1},{1,0},{2,3},{3,2},{4,5},{5,4},{6,7},{7,6},{8,9},{9,8},{10,11... | collective-permute-start | bytes 749576 | tf_op jit(solution)/shard_map/ppermute | solution.py:20
  44.7 23.6 %collective-permute-start.18 = (f32[488,128]{1,0:T(8,128)}, f32[488,128]{1,0:T(8,128)S(1)}, u32[]{:S(2)}, u32[]{:S(2)}) collective-permute-start(f32[488,128]{1,0:T(8,128)} %get-tuple-element.120.refs_1_), channel_id=1, source_target_pairs={{0,1},{1,0},{2,3},{3,2},{4,5},{5,4},{6,7},{7,6},{8,9},{9,8},{10,11... | collective-permute-start | bytes 749576 | tf_op jit(solution)/shard_map/ppermute | solution.py:20
  45.2 9.7 %collective-permute-start.12 = (f32[8,128]{1,0:T(8,128)S(1)}, f32[8,128]{1,0:T(8,128)S(1)}, u32[]{:S(2)}, u32[]{:S(2)}) collective-permute-start(f32[8,128]{1,0:T(8,128)S(1)} %get-tuple-element.118), channel_id=1, source_target_pairs={{0,2},{1,3},{2,0},{3,1},{4,6},{5,7},{6,4},{7,5},{8,10},{9,11},{10,... | collective-permute-start | bytes 12296 | tf_op jit(solution)/shard_map/ppermute | solution.py:20
  54.9 3.6 %collective-permute-start.13 = (f32[8,128]{1,0:T(8,128)S(1)}, f32[8,128]{1,0:T(8,128)S(1)}, u32[]{:S(2)}, u32[]{:S(2)}) collective-permute-start(f32[8,128]{1,0:T(8,128)S(1)} %add.31), channel_id=1, source_target_pairs={{0,4},{4,0},{8,12},{12,8},{16,20},{20,16},{24,28},{28,24},{1,5},{5... | collective-permute-start | bytes 12296 | tf_op jit(solution)/shard_map/ppermute | solution.py:20
  58.5 3.6 %collective-permute-start.14 = (f32[8,128]{1,0:T(8,128)S(1)}, f32[8,128]{1,0:T(8,128)S(1)}, u32[]{:S(2)}, u32[]{:S(2)}) collective-permute-start(f32[8,128]{1,0:T(8,128)S(1)} %add.32), channel_id=1, source_target_pairs={{0,8},{4,12},{8,0},{12,4},{16,24},{20,28},{24,16},{28,20},{1,9},{5... | collective-permute-start | bytes 12296 | tf_op jit(solution)/shard_map/ppermute | solution.py:20
  62.1 7.7 %collective-permute-start.22 = (f32[488,128]{1,0:T(8,128)S(1)}, f32[488,128]{1,0:T(8,128)S(1)}, u32[]{:S(2)}, u32[]{:S(2)}) collective-permute-start(f32[488,128]{1,0:T(8,128)S(1)} %collective-permute-done.20.refs_2_), channel_id=1, source_target_pairs={{0,1},{1,0},{2,3},{3,2},{4,5},{5,4},{6,7},{7,6},{8,9},{9,8},{10,11... | collective-permute-start | bytes 749576 | tf_op jit(solution)/shard_map/ppermute | solution.py:20
  62.1 7.7 %collective-permute-start.21 = (f32[488,128]{1,0:T(8,128)S(1)}, f32[488,128]{1,0:T(8,128)S(1)}, u32[]{:S(2)}, u32[]{:S(2)}) collective-permute-start(f32[488,128]{1,0:T(8,128)S(1)} %collective-permute-done.19.refs_1_), channel_id=1, source_target_pairs={{0,1},{1,0},{2,3},{3,2},{4,5},{5,4},{6,7},{7,6},{8,9},{9,8},{10,11... | collective-permute-start | bytes 749576 | tf_op jit(solution)/shard_map/ppermute | solution.py:20
  62.6 4.5 %collective-permute-start.15 = (f32[8,128]{1,0:T(8,128)S(1)}, f32[8,128]{1,0:T(8,128)S(1)}, u32[]{:S(2)}, u32[]{:S(2)}) collective-permute-start(f32[8,128]{1,0:T(8,128)S(1)} %add.33), channel_id=1, source_target_pairs={{0,16},{4,20},{8,24},{12,28},{16,0},{20,4},{24,8},{28,12},{1,17},{... | collective-permute-start | bytes 12296 | tf_op jit(solution)/shard_map/ppermute | solution.py:20
  67.1 1.2 %collective-permute-start.16 = (f32[8,128]{1,0:T(8,128)S(1)}, f32[8,128]{1,0:T(8,128)S(1)}, u32[]{:S(2)}, u32[]{:S(2)}) collective-permute-start(f32[8,128]{1,0:T(8,128)S(1)} %add.34), channel_id=1, source_target_pairs={{0,1},{1,0},{2,3},{3,2},{4,5},{5,4},{6,7},{7,6},{8,9},{9,8},{10,11... | collective-permute-start | bytes 12296 | tf_op jit(solution)/shard_map/ppermute | solution.py:20
